TPU v7x, 256 devices: a whole 4x4x8 slice. The times are simulated.
256 devices in a mesh: dp: 16 (over y, x), sub: 16 (over z, core).
Axes of the slice: x: 4, y: 4, z: 8, core: 2. Of those that a mesh axis runs over, the one named last changes fastest.
Arguments:
- embeddings: bfloat16 [49152, 1024], P('dp'), may hold values from -4096 to 4096
- assignment: int32 [49152], P('dp'), may hold values from 0 to 4095
- centroids: bfloat16 [4096, 1024], P('sub'), may hold values from -1 to 1
- codebooks: float32 [64, 16, 256], P('sub'), may hold values from -2 to 2
Outputs:
- new_centroids: float32 [4096, 1024], P('sub')
- new_codebooks: float32 [64, 16, 256], P('sub')
All inputs are finite; a program needn't handle non-finite values.
Results may differ from a plain program's by a relative error of at most 0.0004.
The roundings to bfloat16 on the way count: a program that leaves them out, or rounds other values in their place, can miss the bound.
Values may be sent and summed in bfloat16 or wider, within the bound.
A program may use at most 128 MiB of HBM per device.

v0:
```python
import jax
import jax.numpy as jnp
from jax import lax
from jax.sharding import PartitionSpec as P


def from_everyone(x, axis):
    length = lax.axis_size(axis)
    return lax.all_to_all(jnp.broadcast_to(x[None], (length, *x.shape)), axis, 0, 0, tiled=True)


def gathered_once(x, axis):
    leaves = jax.tree.leaves(x)
    sequence = sorted(range(len(leaves)), key=lambda k: -leaves[k].size)
    width = (1, *leaves[sequence[0]].shape)[-1]
    lines = [
        jnp.pad(leaves[k].reshape(-1), (0, -leaves[k].size % width)).reshape(-1, width)
        for k in sequence
    ]
    both, at, found = (from_everyone(jnp.concatenate(lines), axis), 0, {})
    for k, line in zip(sequence, lines):
        share = both[:, at : at + len(line)].reshape(len(both), -1)
        found[k] = share[:, : leaves[k].size].reshape(-1, *leaves[k].shape)
        at += len(line)
    numbers = iter(range(len(leaves)))
    return jax.tree.map(lambda _: found[next(numbers)], x)


def joined_by_halves(pieces, combine):
    while len(jax.tree.leaves(pieces)[0]) > 1:
        pieces = jax.vmap(combine)(
            *(jax.tree.map(lambda part: part[side::2], pieces) for side in (0, 1))
        )
    return jax.tree.map(lambda part: part[0], pieces)


def merged(x, axis, combine):
    pieces = gathered_once(x, axis)
    return joined_by_halves(pieces, combine)


def split_up(x, dim, length):
    lengths = x.shape
    tiles = x.reshape(*lengths[:dim], length, lengths[dim] // length, *lengths[dim + 1 :])
    return jnp.moveaxis(tiles, dim, 0)


def summed_on_arrival(x, axis, dim):
    length = lax.axis_size(axis)
    tiles = lax.all_to_all(split_up(x, dim, length), axis, 0, 0, tiled=True)
    return jnp.sum(tiles, axis=0)


def joined_along(tiles, dim):
    tiles = jnp.moveaxis(tiles, 0, dim)
    lengths = tiles.shape
    return tiles.reshape(*lengths[:dim], lengths[dim] * lengths[dim + 1], *lengths[dim + 2 :])


def collect(x, axis, dim):
    tiles = from_everyone(x, axis)
    return joined_along(tiles, dim)


def taken_together(x, axis):
    everything = from_everyone(x, axis)
    return jnp.sum(everything, axis=0)


def packed_total(arrays, axis):
    ends = [0]
    for a in arrays:
        ends.append(ends[-1] + a.size)
    so_far = taken_together(jnp.concatenate([a.ravel() for a in arrays]), axis)
    return tuple((so_far[b:e].reshape(a.shape) for a, b, e in zip(arrays, ends, ends[1:])))


def merge_softmax(former, latter):
    peak_value = jnp.maximum(former[0], latter[0])
    summed = former[1] * jnp.exp(former[0] - peak_value) + latter[1] * jnp.exp(
        latter[0] - peak_value
    )
    return (peak_value, summed)


def shards(embeddings, assignment, centroids, codebooks):
    feat_width = embeddings.shape[1]
    slice_width = feat_width // lax.axis_size("sub")
    owner_index = lax.axis_index("sub")
    cent_columns = lax.all_to_all(centroids, "sub", split_axis=1, concat_axis=0, tiled=True)
    base_rows = jnp.take(cent_columns, assignment, axis=0).astype(jnp.float32)
    cent_float = centroids.astype(jnp.float32)
    half_norm = 0.5 * jnp.sum(cent_float * cent_float, axis=1)
    logits = (
        jnp.einsum("rd,kd->rk", embeddings, centroids, preferred_element_type=jnp.float32)
        - half_norm[None, :]
    )
    local_peak = jnp.max(logits, axis=1)
    local_total = jnp.sum(jnp.exp(logits - local_peak[:, None]), axis=1)
    peak_value, denominator = merged((local_peak, local_total), "sub", merge_softmax)
    weights = jnp.exp(logits - peak_value[:, None]) / denominator[:, None]
    cent_counts = jnp.sum(weights, axis=0)
    cent_sums = jnp.einsum(
        "rk,rd->kd", weights.astype(jnp.bfloat16), embeddings, preferred_element_type=jnp.float32
    )
    share_sums, share_counts = (
        summed_on_arrival(cent_sums, "dp", 0),
        summed_on_arrival(cent_counts, "dp", 0),
    )
    share_rows = share_sums.shape[0]
    own_rows = lax.dynamic_slice_in_dim(
        cent_float, lax.axis_index("dp") * share_rows, share_rows, 0
    )
    new_share = (share_sums + own_rows) / (share_counts[:, None] + 1.0)
    new_centroids = collect(new_share, "dp", 0)
    row_count = embeddings.shape[0]
    groups = codebooks.shape[0]
    sub_width = codebooks.shape[1]
    own_features = lax.dynamic_slice_in_dim(embeddings, owner_index * slice_width, slice_width, 1)
    residual = own_features.astype(jnp.float32) - base_rows
    res_parts = residual.reshape(row_count, groups, sub_width)
    code_half = 0.5 * jnp.sum(codebooks * codebooks, axis=1)
    code_logits = (
        jnp.einsum("rsd,sdc->rsc", res_parts, codebooks, precision=lax.Precision.HIGHEST)
        - code_half[None]
    )
    code_exp = jnp.exp(code_logits - jnp.max(code_logits, axis=2, keepdims=True))
    code_weights = code_exp / jnp.sum(code_exp, axis=2, keepdims=True)
    code_sums = jnp.einsum("rsc,rsd->sdc", code_weights, res_parts, precision=lax.Precision.HIGHEST)
    code_counts = jnp.sum(code_weights, axis=0)
    code_sums, code_counts = packed_total((code_sums, code_counts), "dp")
    new_codebooks = (code_sums + codebooks) / (code_counts[:, None, :] + 1.0)
    return (new_centroids, new_codebooks)


def solution(mesh):
    placed = (P("dp", None), P("dp"), P("sub", None), P("sub", None, None))
    return jax.shard_map(
        shards,
        mesh=mesh,
        in_specs=placed,
        out_specs=(P("sub", None), P("sub", None, None)),
        check_vma=False,
    )
```

profile of v0, /device:TPU:1, one launch (start us, length us, event | category | flops | bytes accessed | tf_op | source)
XLA Modules:
  0.0 163.9 jit_solution(2008214875265258429)
XLA Ops:
  0.6 1.2 multiply_reduce_fusion
  1.9 4.7 %fusion.12 = (f32[3072]{0:T(1024)S(1)}, f32[3072,256]{0,1:T(8,128)S(1)}) fusion(f32[256]{0:T(256)S(1)} %broadcast_multiply_fusion.1, bf16[3072,1024]{1,0:T(8,128)(2,1)} %param.4, bf16[256,1024]{1,0:T(8,128)(2,1)} %param.6), kind=kOutput, calls=%fused_computation.38 | convolution fusion | flops 1612182528 | bytes 9974784 | tf_op jit(solution)/shard_map/rd,kd->rk/dot_general | solution.py:95
  7.1 0.8 broadcast_in_dim.18
  7.9 10.0 %all-to-all-start = ((f32[16,2,3072]{2,1,0:T(2,128)}), f32[16,2,3072]{2,1,0:T(2,128)S(1)}, u32[]{:S(2)}, u32[]{:S(2)}) async-start(f32[16,2,3072]{2,1,0:T(2,128)} %broadcast_in_dim.18), calls=%async_computation | async-start | bytes 786432 | tf_op jit(solution)/shard_map/all_to_all | solution.py:9
  17.9 2.0 %copy.23 = bf16[256,1024]{0,1:T(8,128)(2,1)} copy(bf16[256,1024]{1,0:T(8,128)(2,1)} %param.6) | data formatting | bytes 1048576 | tf_op args[2]
  19.9 0.9 multiply_reduce_fusion.1
  22.0 10.4 %all-to-all-done = f32[16,2,3072]{2,1,0:T(2,128)S(1)} async-done(((f32[16,2,3072]{2,1,0:T(2,128)}), f32[16,2,3072]{2,1,0:T(2,128)S(1)}, u32[]{:S(2)}, u32[]{:S(2)}) %all-to-all-start) | async-done | bytes 393248 | tf_op jit(solution)/shard_map/all_to_all | solution.py:9
  32.4 4.1 %all-to-all-start.4 = ((bf16[256,16,64]{0,2,1:T(8,128)(2,1)}), bf16[256,16,64]{0,2,1:T(8,128)(2,1)}, u32[]{:S(2)}, u32[]{:S(2)}) async-start(bf16[256,16,64]{0,2,1:T(8,128)(2,1)} %bitcast.41), calls=%async_computation.4 | async-start | bytes 1048576 | tf_op jit(solution)/shard_map/all_to_all | solution.py:90
  38.4 1.0 multiply_add_fusion
  41.2 5.6 %fusion.6 = f32[256,1024]{1,0:T(8,128)} fusion(bf16[3072,1024]{1,0:T(8,128)(2,1)} %param.4, f32[3072,256]{0,1:T(8,128)S(1)} %get-tuple-element.13, f32[3072]{0:T(1024)S(1)} %bitcast.45, f32[3072]{0:T(1024)S(1)} %bitcast.47), kind=kOutput, calls=%fused_computation.12 | convolution fusion | flops 1612972032 | bytes 10510336 | tf_op jit(solution)/shard_map/rk,rd->kd/dot_general | solution.py:103
  46.7 6.3 %all-to-all-done.4 = bf16[256,16,64]{0,2,1:T(8,128)(2,1)} async-done(((bf16[256,16,64]{0,2,1:T(8,128)(2,1)}), bf16[256,16,64]{0,2,1:T(8,128)(2,1)}, u32[]{:S(2)}, u32[]{:S(2)}) %all-to-all-start.4) | async-done | bytes 524320 | tf_op jit(solution)/shard_map/all_to_all | solution.py:90
  53.1 6.8 %all-to-all-start.2 = ((f32[16,1,16]{2,1,0:T(1,128)}), f32[16,1,16]{2,1,0:T(1,128)S(1)}, u32[]{:S(2)}, u32[]{:S(2)}) async-start(f32[16,1,16]{2,1,0:T(1,128)} %all_to_all.35), calls=%async_computation.2 | async-start | bytes 16384 | tf_op jit(solution)/shard_map/all_to_all | solution.py:50
  59.8 1.5 copy.24
  61.4 9.2 %gather_fusion = bf16[3072,64]{1,0:T(8,128)(2,1)S(1)} fusion(bf16[4096,64]{1,0:T(8,128)(2,1)S(1)} %bitcast.37, s32[3072]{0:T(1024)S(1)} %copy-done.4), kind=kCustom, calls=%fused_computation | custom fusion | bytes 798720 | tf_op jit(solution)/shard_map/jit(_take)/gather | solution.py:91
  70.5 2.8 %convert_subtract_fusion = f32[3072,64]{1,0:T(8,128)S(1)} fusion(bf16[3072,64]{1,0:T(8,128)(2,1)S(1)} %gather_fusion, bf16[3072,1024]{1,0:T(8,128)(2,1)} %param.4, s32[]{:T(128)S(6)} %select_n.16, pred[3072]{0:T(1024)(128)(4,1)S(1)} %copy-done.5), kind=kLoop, calls=%fused_computation.11 | loop fusion | flops 786432 | bytes 1575940 | tf_op jit(solution)/shard_map/sub | solution.py:120
  73.8 10.5 %bitcast_reduce_fusion = (f32[3072,4]{0,1:T(4,128)S(1)}, f32[4,3072,256]{1,2,0:T(8,128)S(1)}) fusion(f32[4,256]{1,0:T(4,128)S(1)} %broadcast_multiply_fusion, f32[3072,4,16]{0,2,1:T(8,128)S(1)} %bitcast.39, f32[4,16,256]{2,1,0:T(8,128)S(1)} %copy-done.2), kind=kOutput, calls=%fused_computation.2 | convolution fusion | flops 610258944 | bytes 13488128 | tf_op jit(solution)/shard_map/rsd,sdc->rsc/dot_general | solution.py:124
  84.3 2.9 %fusion.2 = f32[3072,4]{0,1:T(4,128)S(1)} fusion(f32[4,3072,256]{1,2,0:T(8,128)S(1)} %get-tuple-element.15, f32[3072,4]{0,1:T(4,128)S(1)} %get-tuple-element.14, f32[4,256]{1,0:T(4,128)S(1)} %broadcast_multiply_fusion), kind=kLoop, calls=%fused_computation.5 | loop fusion | flops 9424896 | bytes 12685312 | tf_op jit(solution)/shard_map/reduce_sum | solution.py:128
  87.2 1.7 %copy-done = f32[4,3072,256]{1,2,0:T(8,128)} copy-done((f32[4,3072,256]{1,2,0:T(8,128)}, f32[4,3072,256]{1,2,0:T(8,128)S(1)}, u32[]{:S(2)}) %copy-start) | copy-done | bytes 12582936
  88.9 3.5 %fusion.3 = f32[4,256]{1,0:T(4,128)S(1)} fusion(f32[3072,4]{0,1:T(4,128)S(1)} %fusion.2, f32[3072,4]{0,1:T(4,128)S(1)} %get-tuple-element.14, f32[4,3072,256]{1,2,0:T(8,128)S(1)} %get-tuple-element.15, f32[4,256]{1,0:T(4,128)S(1)} %broadcast_multiply_fusion), kind=kLoop, calls=%fused_computation.9 | loop fusion | flops 12581888 | bytes 12689408 | tf_op jit(solution)/shard_map/reduce_sum | solution.py:130
  92.4 6.7 %all-to-all-start.1 = ((f32[16,16,1024]{2,1,0:T(8,128)}), f32[16,16,1024]{2,1,0:T(8,128)S(1)}, u32[]{:S(2)}, u32[]{:S(2)}) async-start(f32[16,16,1024]{2,1,0:T(8,128)} %bitcast.5), calls=%async_computation.1 | async-start | bytes 2097152 | tf_op jit(solution)/shard_map/all_to_all | solution.py:50
  99.1 14.6 %fusion.4 = f32[4,16,256]{2,1,0:T(8,128)S(1)} fusion(f32[3072,4,16]{0,2,1:T(8,128)S(1)} %bitcast.40, f32[4,3072,256]{1,2,0:T(8,128)} %copy-done, f32[3072,4]{0,1:T(4,128)S(1)} %fusion.2, f32[3072,4]{0,1:T(4,128)S(1)} %get-tuple-element.14, f32[4,256]{1,0:T(4,128)S(1)} %broadcast_multiply_fusion), kind=kOutput, calls=%fused_computation.10 | convolution fusion | flops 613416960 | bytes 13537280 | tf_op jit(solution)/shard_map/rsc,rsd->sdc/dot_general | solution.py:129
  113.8 5.2 %all-to-all-done.1 = f32[16,16,1024]{2,1,0:T(8,128)S(1)} async-done(((f32[16,16,1024]{2,1,0:T(8,128)}), f32[16,16,1024]{2,1,0:T(8,128)S(1)}, u32[]{:S(2)}, u32[]{:S(2)}) %all-to-all-start.1) | async-done | bytes 1048608 | tf_op jit(solution)/shard_map/all_to_all | solution.py:50
  119.0 1.6 broadcast_in_dim.23
  120.5 3.7 %all-to-all-start.5 = ((f32[16,1,17408]{2,1,0:T(1,128)}), f32[16,1,17408]{2,1,0:T(1,128)S(1)}, u32[]{:S(2)}, u32[]{:S(2)}) async-start(f32[16,1,17408]{2,1,0:T(1,128)} %broadcast_in_dim.23), calls=%async_computation.5 | async-start | bytes 2228224 | tf_op jit(solution)/shard_map/all_to_all | solution.py:9
  124.3 1.1 convert_element_type.12
  125.4 0.9 add_divide_fusion.1
  126.4 15.0 %all-to-all-done.5 = f32[16,1,17408]{2,1,0:T(1,128)S(1)} async-done(((f32[16,1,17408]{2,1,0:T(1,128)}), f32[16,1,17408]{2,1,0:T(1,128)S(1)}, u32[]{:S(2)}, u32[]{:S(2)}) %all-to-all-start.5) | async-done | bytes 1114144 | tf_op jit(solution)/shard_map/all_to_all | solution.py:9
  141.4 1.1 broadcast_in_dim.19
  142.5 4.7 %all-to-all-start.3 = ((f32[16,16,1024]{2,1,0:T(8,128)}), f32[16,16,1024]{2,1,0:T(8,128)S(1)}, u32[]{:S(2)}, u32[]{:S(2)}) async-start(f32[16,16,1024]{2,1,0:T(8,128)} %broadcast_in_dim.19), calls=%async_computation.3 | async-start | bytes 2097152 | tf_op jit(solution)/shard_map/all_to_all | solution.py:9
  147.1 0.7 reduce_sum.89
  148.6 14.4 %all-to-all-done.3 = f32[16,16,1024]{2,1,0:T(8,128)S(1)} async-done(((f32[16,16,1024]{2,1,0:T(8,128)}), f32[16,16,1024]{2,1,0:T(8,128)S(1)}, u32[]{:S(2)}, u32[]{:S(2)}) %all-to-all-start.3) | async-done | bytes 1048608 | tf_op jit(solution)/shard_map/all_to_all | solution.py:9
  162.9 1.0 copy.39
  (49 shorter events, 6.5 us)
Async XLA Ops:
  1.9 18.9 %copy-start.3 = (s32[3072]{0:T(1024)S(1)}, s32[3072]{0:T(1024)}, u32[]{:S(2)}) copy-start(s32[3072]{0:T(1024)} %param.5) | copy-start | bytes 36868
  7.9 24.5 %all-to-all-start = ((f32[16,2,3072]{2,1,0:T(2,128)}), f32[16,2,3072]{2,1,0:T(2,128)S(1)}, u32[]{:S(2)}, u32[]{:S(2)}) async-start(f32[16,2,3072]{2,1,0:T(2,128)} %broadcast_in_dim.18), calls=%async_computation | async-start | bytes 786432 | tf_op jit(solution)/shard_map/all_to_all | solution.py:9
  32.4 20.6 %all-to-all-start.4 = ((bf16[256,16,64]{0,2,1:T(8,128)(2,1)}), bf16[256,16,64]{0,2,1:T(8,128)(2,1)}, u32[]{:S(2)}, u32[]{:S(2)}) async-start(bf16[256,16,64]{0,2,1:T(8,128)(2,1)} %bitcast.41), calls=%async_computation.4 | async-start | bytes 1048576 | tf_op jit(solution)/shard_map/all_to_all | solution.py:90
  41.2 20.2 %copy-start.4 = (s32[3072]{0:T(1024)S(1)}, s32[3072]{0:T(1024)}, u32[]{:S(2)}) copy-start(s32[3072]{0:T(1024)} %fusion.10) | copy-start | bytes 36868
  46.7 23.8 %copy-start.5 = (pred[3072]{0:T(1024)(128)(4,1)S(1)}, pred[3072]{0:T(1024)(128)(4,1)}, u32[]{:S(2)}) copy-start(pred[3072]{0:T(1024)(128)(4,1)} %compare_and_fusion) | copy-start | bytes 9220
  53.1 39.3 %all-to-all-start.2 = ((f32[16,1,16]{2,1,0:T(1,128)}), f32[16,1,16]{2,1,0:T(1,128)S(1)}, u32[]{:S(2)}, u32[]{:S(2)}) async-start(f32[16,1,16]{2,1,0:T(1,128)} %all_to_all.35), calls=%async_computation.2 | async-start | bytes 16384 | tf_op jit(solution)/shard_map/all_to_all | solution.py:50
  61.4 12.5 %copy-start.2 = (f32[4,16,256]{2,1,0:T(8,128)S(1)}, f32[4,16,256]{2,1,0:T(8,128)}, u32[]{:S(2)}) copy-start(f32[4,16,256]{2,1,0:T(8,128)} %param.7) | copy-start | bytes 196612
  84.3 4.6 %copy-start = (f32[4,3072,256]{1,2,0:T(8,128)}, f32[4,3072,256]{1,2,0:T(8,128)S(1)}, u32[]{:S(2)}) copy-start(f32[4,3072,256]{1,2,0:T(8,128)S(1)} %get-tuple-element.15) | copy-start | bytes 37748740
  92.4 26.6 %all-to-all-start.1 = ((f32[16,16,1024]{2,1,0:T(8,128)}), f32[16,16,1024]{2,1,0:T(8,128)S(1)}, u32[]{:S(2)}, u32[]{:S(2)}) async-start(f32[16,16,1024]{2,1,0:T(8,128)} %bitcast.5), calls=%async_computation.1 | async-start | bytes 2097152 | tf_op jit(solution)/shard_map/all_to_all | solution.py:50
  99.1 25.2 %copy-start.1 = (bf16[256,1024]{1,0:T(8,128)(2,1)S(1)}, bf16[256,1024]{1,0:T(8,128)(2,1)}, u32[]{:S(2)}) copy-start(bf16[256,1024]{1,0:T(8,128)(2,1)} %param.6) | copy-start | bytes 1572868
  120.5 20.8 %all-to-all-start.5 = ((f32[16,1,17408]{2,1,0:T(1,128)}), f32[16,1,17408]{2,1,0:T(1,128)S(1)}, u32[]{:S(2)}, u32[]{:S(2)}) async-start(f32[16,1,17408]{2,1,0:T(1,128)} %broadcast_in_dim.23), calls=%async_computation.5 | async-start | bytes 2228224 | tf_op jit(solution)/shard_map/all_to_all | solution.py:9
  142.5 20.5 %all-to-all-start.3 = ((f32[16,16,1024]{2,1,0:T(8,128)}), f32[16,16,1024]{2,1,0:T(8,128)S(1)}, u32[]{:S(2)}, u32[]{:S(2)}) async-start(f32[16,16,1024]{2,1,0:T(8,128)} %broadcast_in_dim.19), calls=%async_computation.3 | async-start | bytes 2097152 | tf_op jit(solution)/shard_map/all_to_all | solution.py:9
where the time goes:
time: 165 us; the launch traced here: 164 us
  waiting for transfers between devices  51.4 us (31%)
  starting transfers between devices  35.9 us (22%)
  matrix products  35.4 us (21%)
  local copies, waits for them, and re-layouts  22.2 us (13%)
  other arithmetic  18.1 us (11%)
    all_to_all x3, waiting for transfers between devices, from_everyone(): lax.all_to_all(jnp.broadcast_to(x[None], (length, *x.shape)), axis, 0, 0,...  39.8 us
    all_to_all x3, starting transfers between devices, from_everyone(): lax.all_to_all(jnp.broadcast_to(x[None], (length, *x.shape)), axis, 0, 0,...  18.4 us
    dot_general x1, matrix products, shards(): jnp.einsum('rsc,rsd->sdc', code_weights, res_parts, precision=lax.Precisi...  14.6 us
    all_to_all x2, starting transfers between devices, summed_on_arrival(): tiles = lax.all_to_all(split_up(x, dim, length), axis, 0, 0, tiled=True)  13.4 us
    dot_general x1, matrix products, shards(): jnp.einsum('rsd,sdc->rsc', res_parts, codebooks, precision=lax.Precision....  10.5 us
    gather x1, local copies, waits for them, and re-layouts, shards(): base_rows = jnp.take(cent_columns, assignment, axis=0).astype(jnp.float32)  9.16 us
    all_to_all x1, waiting for transfers between devices, shards(): lax.all_to_all(centroids, 'sub', split_axis=1, concat_axis=0, tiled=True)  6.31 us
    dot_general x1, matrix products, shards(): jnp.einsum('rk,rd->kd', weights.astype(jnp.bfloat16), embeddings, preferr...  5.56 us
  transfers between devices with their start and end apart: 6, of which 5 were waited for; matrix products, arithmetic and copies ran while one was open for 38% of the time, Pallas kernels for 0%

commit v1 on v0

v1 whole, which is shorter than its diff:
```python
import jax
import jax.numpy as jnp
from jax import lax
from jax.experimental import pallas as pl
from jax.experimental.pallas import tpu as pltpu
from jax.sharding import PartitionSpec as P

R, D, KL = 3072, 1024, 256
NC, RC = 6, 512
CH = 256
F32, BF16 = jnp.float32, jnp.bfloat16
LOG2E = 1.4426950408889634


def rcopy(src, dst, ssem, rsem, **where):
    return pltpu.make_async_remote_copy(
        src_ref=src, dst_ref=dst, send_sem=ssem, recv_sem=rsem,
        device_id=where, device_id_type=pl.DeviceIdType.MESH,
    )


def split3(v):
    a = v.astype(BF16).astype(F32)
    r = v - a
    b = r.astype(BF16).astype(F32)
    return a, b, (r - b).astype(BF16).astype(F32)


def kernel(
    emb_hbm, asg_hbm, cent_hbm, cb_hbm, out_ref, cbo_ref,
    emb, asg, cent, cb, eT, wT, st, rs, fs, zbuf, tb, tf, xg, embT, cenT, cbt,
    sums, r1, s1, r2, cg, cc, acc, accT, cs, cr,
    lsem, zs, zr, ts, tr, ps, pr, ss, sr, gs, gr, ns, nr, xs, xr, ks, kr, os, orr,
):
    dp = lax.axis_index("dp")
    sub = lax.axis_index("sub")
    y, x = dp // 4, dp % 4
    z, c = sub // 2, sub % 2
    sends = []

    lc = pltpu.make_async_copy(cent_hbm, cent, lsem.at[6])
    lb = pltpu.make_async_copy(cb_hbm, cb, lsem.at[7])
    la = pltpu.make_async_copy(asg_hbm, asg, lsem.at[8])
    lc.start()
    loads = []
    for k in range(NC):
        sl = pl.ds(k * RC, RC)
        cp = pltpu.make_async_copy(emb_hbm.at[sl, :], emb.at[sl, :], lsem.at[k])
        cp.start()
        loads.append(cp)
    lb.start()
    la.start()

    bar = pltpu.get_barrier_semaphore()
    for k in range(1, 16):
        pl.semaphore_signal(bar, inc=1, device_id={"sub": (sub + k) % 16}, device_id_type=pl.DeviceIdType.MESH)
        pl.semaphore_signal(bar, inc=1, device_id={"dp": (dp + k) % 16}, device_id_type=pl.DeviceIdType.MESH)
    st[...] = jnp.ones(st.shape, F32)
    acc[...] = jnp.zeros(acc.shape, F32)
    lc.wait()
    pl.semaphore_wait(bar, 30)

    zc = []
    rows16 = pl.ds(pl.multiple_of(dp * 16, 16), 16)
    for k in range(1, 8):
        zz = (z + k) % 8
        cp = rcopy(cent.at[rows16, pl.ds(pl.multiple_of(zz * 128, 128), 128)], zbuf.at[z],
                   zs.at[k], zr.at[k], sub=zz * 2 + c)
        cp.start()
        zc.append(cp)
    lanes128 = pl.ds(pl.multiple_of(z * 128, 128), 128)
    zbuf[z] = cent[rows16, lanes128]

    cf = cent[...].astype(F32)
    hn = 0.5 * jnp.sum(cf * cf, axis=1, keepdims=True)
    tc = []
    for k in range(NC):
        loads[k].wait()
        l = lax.dot_general(cent[...], emb[k * RC:(k + 1) * RC, :], (((1,), (1,)), ((), ())),
                            preferred_element_type=F32) - hn
        m = jnp.max(l, axis=0, keepdims=True)
        e = jnp.exp(l - m)
        s = jnp.sum(e, axis=0, keepdims=True)
        eT[:, k * RC:(k + 1) * RC] = e
        for i in range(RC // 128):
            r = k * (RC // 128) + i
            st[r % 16, pl.ds(r // 16, 1), :] = m[:, i * 128:(i + 1) * 128]
            st[r % 16, pl.ds(2 + r // 16, 1), :] = s[:, i * 128:(i + 1) * 128]
        if k == 2:
            for cp in zc:
                cp.wait()
            tb[:, c, dp] = zbuf[...]
            for j in range(1, 16):
                cp = rcopy(zbuf, tb.at[:, c, dp], ts.at[j], tr.at[j], dp=(dp + j) % 16)
                cp.start()
                tc.append(cp)

    sc_ = []
    for k in range(1, 16):
        o = (sub + k) % 16
        cp = rcopy(st.at[o], rs.at[sub], ss.at[k], sr.at[k], sub=o)
        cp.start()
        sc_.append(cp)
    rs[sub] = st[sub]

    lb.wait()
    for s in range(4):
        v = cb[s]
        parts = split3(v * LOG2E)
        half = split3(-0.5 * LOG2E * jnp.sum(v * v, axis=0, keepdims=True))
        neg = tuple(-p for p in parts)
        stack = jnp.concatenate(parts + neg + half + (jnp.zeros((29, 256), F32),), axis=0)
        cbt[s] = jnp.transpose(stack).astype(BF16)

    for cp in sc_:
        cp.wait()
    v = rs[...]
    big = jnp.max(v[:, 0:2], axis=0)
    tot = jnp.sum(v[:, 2:4] * jnp.exp(v[:, 0:2] - big[None]), axis=0)
    fs[sub, 0:2, :] = big
    fs[sub, 2:4, :] = tot
    fc = []
    for k in range(1, 16):
        cp = rcopy(fs.at[sub], fs.at[sub], gs.at[k], gr.at[k], sub=(sub + k) % 16)
        cp.start()
        fc.append(cp)

    def turn(k, _):
        o = pl.multiple_of(k * RC, RC)
        embT[:, pl.ds(o, RC)] = jnp.transpose(emb[pl.ds(o, RC), lanes128].astype(F32)).astype(BF16)
        return 0
    lax.fori_loop(0, NC, turn, 0)

    for cp in fc:
        cp.wait()
    cp_ = jnp.zeros((KL, 128), F32)
    for k in range(NC):
        scale = []
        for i in range(RC // 128):
            r = k * (RC // 128) + i
            a, b = r % 16, r // 16
            scale.append(jnp.exp(st[a, pl.ds(b, 1), :] - fs[a, pl.ds(b, 1), :]) / fs[a, pl.ds(2 + b, 1), :])
        p = eT[:, k * RC:(k + 1) * RC] * jnp.concatenate(scale, axis=1)
        for i in range(RC // 128):
            cp_ = cp_ + p[:, i * 128:(i + 1) * 128]
        wT[:, k * RC:(k + 1) * RC] = p.astype(BF16)

    ax = [(x, y), (x, y), (y, x), (y, x)]

    def peer(q, first, k):
        ix, iy = x, y
        if (q < 2) == first:
            ix = (x + k) % 4
        else:
            iy = (y + k) % 4
        return iy * 4 + ix, (ix if (q < 2) == first else iy)

    c1 = [[] for _ in range(4)]
    for q in range(4):
        sums[q] = jnp.dot(wT[...], emb[:, q * 256:(q + 1) * 256], preferred_element_type=F32)
        for k in range(1, 4):
            dev, pa = peer(q, True, k)
            cp = rcopy(sums.at[q, pl.ds(pl.multiple_of(pa * 64, 64), 64), :], r1.at[q, k - 1],
                       xs.at[0, q, k], xr.at[0, q, k], dp=dev)
            cp.start()
            c1[q].append(cp)

    cg[dp] = jnp.broadcast_to(jnp.sum(jnp.transpose(cp_), axis=0, keepdims=True), (8, 256))
    nc = []
    for k in range(1, 16):
        cp = rcopy(cg.at[dp], cg.at[dp], ns.at[k], nr.at[k], dp=(dp + k) % 16)
        cp.start()
        nc.append(cp)

    for cp in tc:
        cp.wait()
    cp = rcopy(tb.at[:, c], tb.at[:, c], ps.at[0], pr.at[0], sub=z * 2 + (1 - c))
    cp.start()
    cp.wait()
    la.wait()

    def widen(i, _):
        tf[pl.ds(pl.multiple_of(i * 256, 256), 256), :] = tb[i // 2, i % 2].reshape(256, 128).astype(F32)
        return 0
    lax.fori_loop(0, 16, widen, 0)

    def fetch(i, _):
        o = pl.multiple_of(i * 16, 16)
        for j in range(16):
            xg[pl.ds(o + j, 1), :] = tf[pl.ds(asg[o + j], 1), :]
        return 0
    lax.fori_loop(0, R // 16, fetch, 0)

    c2 = [[] for _ in range(4)]
    for q in range(4):
        for cp in c1[q]:
            cp.wait()
        a, b = ax[q]
        s1[q] = sums[q, pl.ds(pl.multiple_of(a * 64, 64), 64), :] + r1[q, 0] + r1[q, 1] + r1[q, 2]
        for k in range(1, 4):
            dev, pb = peer(q, False, k)
            cp = rcopy(s1.at[q, pl.ds(pl.multiple_of(pb * 16, 16), 16), :], r2.at[q, k - 1],
                       xs.at[1, q, k], xr.at[1, q, k], dp=dev)
            cp.start()
            c2[q].append(cp)

    mine = (lax.broadcasted_iota(jnp.int32, (RC, 128), 1) // 64) == c

    def turn2(k, _):
        o = pl.multiple_of(k * RC, RC)
        g = xg[pl.ds(o, RC), :]
        cenT[:, pl.ds(o, RC)] = jnp.transpose(g).astype(BF16)
        xg[pl.ds(o, RC), :] = jnp.where(mine, g, 1.0)
        return 0
    lax.fori_loop(0, NC, turn2, 0)

    feats = pl.ds(pl.multiple_of(c * 64, 64), 64)

    def code(k, _):
        o = pl.multiple_of(k * CH, CH)
        et = embT[feats, pl.ds(o, CH)]
        ct = cenT[feats, pl.ds(o, CH)]
        xr_ = jnp.concatenate([emb[pl.ds(o, CH), lanes128], xg[pl.ds(o, CH), :].astype(BF16)], axis=1)
        one = jnp.ones((16, CH), BF16)
        for s in range(4):
            es, cs_ = et[16 * s:16 * s + 16], ct[16 * s:16 * s + 16]
            xt = jnp.concatenate([es, es, es, cs_, cs_, cs_, one, one], axis=0)
            l = jnp.dot(cbt[s], xt, preferred_element_type=F32)
            e = jnp.exp2(l - jnp.max(l, axis=0, keepdims=True))
            w = e * (1.0 / jnp.sum(e, axis=0, keepdims=True))
            hi = w.astype(BF16)
            lo = (w - hi.astype(F32)).astype(BF16)
            acc[s] += jnp.dot(hi, xr_, preferred_element_type=F32) + jnp.dot(lo, xr_, preferred_element_type=F32)
        return 0

    lax.fori_loop(0, 4, code, 0)

    for cp in nc:
        cp.wait()
    ctot = jnp.sum(cg[...], axis=0)[0:1]
    cc[...] = jnp.transpose(jnp.broadcast_to(ctot, (128, 256))) + 1.0
    c3 = [[] for _ in range(4)]
    for q in range(4):
        for cp in c2[q]:
            cp.wait()
        a, b = ax[q]
        row = pl.ds(pl.multiple_of(a * 64 + b * 16, 16), 16)
        qs = slice(q * 256, (q + 1) * 256)
        fin = s1[q, pl.ds(pl.multiple_of(b * 16, 16), 16), :] + r2[q, 0] + r2[q, 1] + r2[q, 2]
        den = cc[row, :]
        out_ref[row, qs] = (fin + cent[row, qs].astype(F32)) / jnp.concatenate([den, den], axis=1)
        for k in range(1, 4):
            dev, _ = peer(q, False, k)
            piece = out_ref.at[row, pl.ds(q * 256, 256)]
            cp = rcopy(piece, piece, xs.at[2, q, k], xr.at[2, q, k], dp=dev)
            cp.start()
            c3[q].append(cp)

    lax.fori_loop(4, 7, code, 0)

    c4 = []
    for q in range(4):
        for cp in c3[q]:
            cp.wait()
        a, b = ax[q]
        for k in range(1, 4):
            dev, _ = peer(q, True, k)
            piece = out_ref.at[pl.ds(pl.multiple_of(a * 64, 64), 64), pl.ds(q * 256, 256)]
            cp = rcopy(piece, piece, xs.at[3, q, k], xr.at[3, q, k], dp=dev)
            cp.start()
            c4.append(cp)

    lax.fori_loop(7, R // CH, code, 0)

    for s in range(4):
        accT[...] = jnp.transpose(acc[s])
        f = pl.multiple_of(c * 64 + s * 16, 16)
        tot16 = accT[pl.ds(f, 16), :] - accT[pl.ds(pl.multiple_of(128 + f, 16), 16), :]
        cnt = accT[pl.ds(pl.multiple_of(128 + (1 - c) * 64, 64), 8), :]
        for h in range(2):
            for g in range(2):
                cs[s * 4 + h * 2 + g, 0:8, :] = tot16[8 * g:8 * g + 8, 128 * h:128 * h + 128]
                cs[s * 4 + h * 2 + g, 8:16, :] = cnt[:, 128 * h:128 * h + 128]
    kc = []
    for k in range(1, 16):
        o = (dp + k) % 16
        cp = rcopy(cs.at[o], cr.at[dp], ks.at[k], kr.at[k], dp=o)
        cp.start()
        kc.append(cp)
    cr[dp] = cs[dp]
    for cp in kc:
        cp.wait()
    t = jnp.sum(cr[...], axis=0)
    so, ho, go = dp // 4, (dp // 2) % 2, dp % 2
    g8 = pl.ds(pl.multiple_of(go * 8, 8), 8)
    h128 = pl.ds(pl.multiple_of(ho * 128, 128), 128)
    cbo_ref[so, g8, h128] = (t[0:8] + cb[so, g8, h128]) / (t[8:16] + 1.0)
    oc = []
    for k in range(1, 16):
        piece = cbo_ref.at[so, g8, h128]
        cp = rcopy(piece, piece, os.at[k], orr.at[k], dp=(dp + k) % 16)
        cp.start()
        oc.append(cp)
    for cp in c4 + oc:
        cp.wait()


def shards(embeddings, assignment, centroids, codebooks):
    dma = pltpu.SemaphoreType.DMA
    v = pltpu.VMEM
    hbm = pl.BlockSpec(memory_space=pl.ANY)
    vm = pl.BlockSpec(memory_space=pltpu.VMEM)
    return pl.pallas_call(
        kernel,
        out_shape=(jax.ShapeDtypeStruct((KL, D), F32), jax.ShapeDtypeStruct((4, 16, 256), F32)),
        in_specs=[hbm] * 4,
        out_specs=(vm, vm),
        scratch_shapes=[
            v((R, D), BF16), pltpu.SMEM((R,), jnp.int32), v((KL, D), BF16), v((4, 16, 256), F32),
            v((KL, R), F32), v((KL, R), BF16),
            v((16, 8, 128), F32), v((16, 8, 128), F32), v((16, 8, 128), F32),
            v((8, 16, 128), BF16), v((8, 2, 16, 16, 128), BF16), v((4096, 128), F32), v((R, 128), F32),
            v((128, R), BF16), v((128, R), BF16), v((4, 256, 128), BF16),
            v((4, 256, 256), F32), v((4, 3, 64, 256), F32), v((4, 64, 256), F32), v((4, 3, 16, 256), F32),
            v((16, 8, 256), F32), v((256, 128), F32), v((4, 256, 256), F32), v((256, 256), F32),
            v((16, 16, 128), F32), v((16, 16, 128), F32),
            dma((9,)), dma((8,)), dma((8,)), dma((16,)), dma((16,)), dma((1,)), dma((1,)),
            dma((16,)), dma((16,)), dma((16,)), dma((16,)), dma((16,)), dma((16,)),
            dma((4, 4, 4)), dma((4, 4, 4)), dma((16,)), dma((16,)), dma((16,)), dma((16,)),
        ],
        compiler_params=pltpu.CompilerParams(
            collective_id=0, has_side_effects=True, vmem_limit_bytes=52 * 1024 * 1024),
        name="step",
    )(embeddings, assignment, centroids, codebooks)


def solution(mesh):
    placed = (P("dp", None), P("dp"), P("sub", None), P("sub", None, None))
    return jax.shard_map(
        shards,
        mesh=mesh,
        in_specs=placed,
        out_specs=(P("sub", None), P("sub", None, None)),
        check_vma=False,
    )
```

time: 165 us -> 71.9 us (0.44)
  the two profiles are of different devices: /device:TPU:1 before, /device:TPU:8 now
where the time goes in v1:
time: 71.9 us; the launch traced here: 71.7 us
  Pallas kernels  66.8 us (93%)
  local copies, waits for them, and re-layouts  4.18 us (6%)
    pallas_call x1, Pallas kernels, shards(): pl.pallas_call(kernel, out_shape=(jax.ShapeDtypeStruct((KL, D), F32), jax...  66.8 us
    unnamed x8, local copies, waits for them, and re-layouts  4.18 us

profile of v1, /device:TPU:8, one launch (start us, length us, event | category | flops | bytes accessed | tf_op | source)
XLA Modules:
  0.0 71.7 jit_solution(14957737609022900056)
XLA Ops:
  0.6 0.0 copy-start
  0.6 1.0 %copy-done = bf16[256,1024]{1,0:T(8,128)(2,1)S(1)} copy-done((bf16[256,1024]{1,0:T(8,128)(2,1)S(1)}, bf16[256,1024]{1,0:T(8,128)(2,1)}, u32[]{:S(2)}) %copy-start) | copy-done | bytes 524312
  1.7 0.0 copy-start.1
  1.7 0.8 %copy-done.1 = f32[4,16,256]{2,1,0:T(8,128)S(1)} copy-done((f32[4,16,256]{2,1,0:T(8,128)S(1)}, f32[4,16,256]{2,1,0:T(8,128)}, u32[]{:S(2)}) %copy-start.1) | copy-done | bytes 65560
  2.5 0.0 copy-start.2
  2.5 0.7 copy-done.2
  3.2 66.8 %step.1 = (f32[256,1024]{1,0:T(8,128)S(1)}, f32[4,16,256]{2,1,0:T(8,128)S(1)}) custom-call(bf16[3072,1024]{1,0:T(8,128)(2,1)} %emb_hbm.1, s32[3072]{0:T(1024)S(1)} %copy-done.2, bf16[256,1024]{1,0:T(8,128)(2,1)S(1)} %copy-done, f32[4,16,256]{2,1,0:T(8,128)S(1)} %copy-done.1), custom_call_target="tpu_custom_call" | custom-call | tf_op jit(solution)/shard_map/step/pallas_call | solution.py:313
  70.1 1.0 %copy.8 = f32[256,1024]{1,0:T(8,128)} copy(f32[256,1024]{1,0:T(8,128)S(1)} %get-tuple-element.4) | data formatting | bytes 2097152
  71.0 0.6 copy.9
Async XLA Ops:
  0.6 1.0 %copy-start = (bf16[256,1024]{1,0:T(8,128)(2,1)S(1)}, bf16[256,1024]{1,0:T(8,128)(2,1)}, u32[]{:S(2)}) copy-start(bf16[256,1024]{1,0:T(8,128)(2,1)} %cent_hbm.1) | copy-start | bytes 1572868
  1.7 0.8 %copy-start.1 = (f32[4,16,256]{2,1,0:T(8,128)S(1)}, f32[4,16,256]{2,1,0:T(8,128)}, u32[]{:S(2)}) copy-start(f32[4,16,256]{2,1,0:T(8,128)} %cb_hbm.1) | copy-start | bytes 196612
  2.5 0.7 copy-start.2

commit v2 on v0

v2 whole, which is shorter than its diff:
```python
import jax
import jax.numpy as jnp
from jax import lax
from jax.experimental import pallas as pl
from jax.experimental.pallas import tpu as pltpu
from jax.sharding import PartitionSpec as P

R, D, KL = 3072, 1024, 256
NC, RC = 6, 512
F32, BF16 = jnp.float32, jnp.bfloat16
LOG2E = 1.4426950408889634


def rcopy(src, dst, ssem, rsem, **where):
    return pltpu.make_async_remote_copy(
        src_ref=src, dst_ref=dst, send_sem=ssem, recv_sem=rsem,
        device_id=where, device_id_type=pl.DeviceIdType.MESH,
    )


def split3(v):
    a = v.astype(BF16).astype(F32)
    r = v - a
    b = r.astype(BF16).astype(F32)
    return a, b, (r - b).astype(BF16).astype(F32)


def kernel(
    emb_hbm, asg_hbm, cent_hbm, cb_hbm, out_ref, cbo_ref,
    emb, asg, cent, cb, eT, wT, st, ra, mz, fs, scl, zbuf, tb, tf, xg, embT, cenT, cbt,
    sums, r1, s1, r2, cg, cc, acc, accT, cs, cr, xgb, lsc, wh,
    lsem, zs, zr, ts, tr, ps, pr, ss, sr, gs, gr, ns, nr, xs, xr, ks, kr, os, orr,
):
    dp = lax.axis_index("dp")
    sub = lax.axis_index("sub")
    y, x = dp // 4, dp % 4
    z, c = sub // 2, sub % 2

    with jax.named_scope("load"):
        lc = pltpu.make_async_copy(cent_hbm, cent, lsem.at[6])
        lb = pltpu.make_async_copy(cb_hbm, cb, lsem.at[7])
        la = pltpu.make_async_copy(asg_hbm, asg, lsem.at[8])
        lc.start()
        loads = []
        for k in range(3):
            sl = pl.ds(k * 1024, 1024)
            cp = pltpu.make_async_copy(emb_hbm.at[sl, :], emb.at[sl, :], lsem.at[k])
            cp.start()
            loads.append(cp)
        lb.start()
        la.start()
        bar = pltpu.get_barrier_semaphore()
        for k in range(1, 16):
            pl.semaphore_signal(bar, inc=1, device_id={"sub": (sub + k) % 16}, device_id_type=pl.DeviceIdType.MESH)
            pl.semaphore_signal(bar, inc=1, device_id={"dp": (dp + k) % 16}, device_id_type=pl.DeviceIdType.MESH)
        acc[...] = jnp.zeros(acc.shape, F32)
        rows16 = pl.ds(pl.multiple_of(dp * 16, 16), 16)
        lanes128 = pl.ds(pl.multiple_of(z * 128, 128), 128)
        lc.wait()
        zbuf[z] = cent[rows16, lanes128]

    with jax.named_scope("logits"):
        cf = cent[...].astype(F32)
        hn = 0.5 * jnp.sum(cf * cf, axis=1, keepdims=True)
        for k in range(NC):
            if k % 2 == 0:
                loads[k // 2].wait()
            l = lax.dot_general(cent[...], emb[k * RC:(k + 1) * RC, :], (((1,), (1,)), ((), ())),
                                preferred_element_type=F32) - hn
            m = jnp.max(l, axis=0, keepdims=True)
            e = jnp.exp(l - m)
            s = jnp.sum(e, axis=0, keepdims=True)
            eT[:, k * RC:(k + 1) * RC] = e
            for i in range(RC // 128):
                h, r = divmod(k * (RC // 128) + i, 12)
                st[h, r:r + 1, :] = m[:, i * 128:(i + 1) * 128]
                st[h, 12 + r:13 + r, :] = s[:, i * 128:(i + 1) * 128]

    with jax.named_scope("barrier"):
        pl.semaphore_wait(bar, 30)
    with jax.named_scope("statsend"):
        other = z * 2 + (1 - c)
        ca = rcopy(st.at[1 - c], ra, ss.at[0], sr.at[0], sub=other)
        ca.start()
    with jax.named_scope("zsend"):
        zc = []
        for k in range(1, 8):
            zz = (z + k) % 8
            cp = rcopy(cent.at[rows16, pl.ds(pl.multiple_of(zz * 128, 128), 128)], zbuf.at[z],
                       zs.at[k], zr.at[k], sub=zz * 2 + c)
            cp.start()
            zc.append(cp)
    with jax.named_scope("cbprep"):
        lb.wait()
        for s in range(4):
            v = cb[s]
            parts = split3(v * LOG2E)
            half = split3(-0.5 * LOG2E * jnp.sum(v * v, axis=0, keepdims=True))
            neg = tuple(-p for p in parts)
            stack = jnp.concatenate(parts + neg + half + (jnp.zeros((29, 256), F32),), axis=0)
            cbt[s] = jnp.transpose(stack).astype(BF16)
        for k in range(NC):
            o = k * RC
            embT[:, pl.ds(o, RC)] = jnp.transpose(emb[pl.ds(o, RC), lanes128].astype(F32)).astype(BF16)

    with jax.named_scope("statwait"):
        ca.wait()
    with jax.named_scope("merge"):
        ma, mb = st[c, 0:12, :], ra[0:12, :]
        big = jnp.maximum(ma, mb)
        mz[z, 0:12, :] = big
        mz[z, 12:24, :] = st[c, 12:24, :] * jnp.exp(ma - big) + ra[12:24, :] * jnp.exp(mb - big)
        bc = []
        for k in range(1, 8):
            cp = rcopy(mz.at[z], mz.at[z], gs.at[k], gr.at[k], sub=((z + k) % 8) * 2 + c)
            cp.start()
            bc.append(cp)
    with jax.named_scope("zwait"):
        for cp in zc:
            cp.wait()
    with jax.named_scope("tabsend"):
        tb[:, c, dp] = zbuf[...]
        tc = []
        for j in range(1, 16):
            cp = rcopy(zbuf, tb.at[:, c, dp], ts.at[j], tr.at[j], dp=(dp + j) % 16)
            cp.start()
            tc.append(cp)
    with jax.named_scope("finwait"):
        for cp in bc:
            cp.wait()
    with jax.named_scope("merge2"):
        mv = mz[:, 0:12, :]
        big = jnp.max(mv, axis=0)
        fs[c, 0:12, :] = big
        fs[c, 12:24, :] = jnp.sum(mz[:, 12:24, :] * jnp.exp(mv - big[None]), axis=0)
        cp = rcopy(fs.at[c], fs.at[c], ss.at[1], sr.at[1], sub=other)
        cp.start()
        cp.wait()
    with jax.named_scope("weights"):
        cp_ = jnp.zeros((KL, 128), F32)
        for h in range(2):
            scl[h] = jnp.exp(st[h, 0:12, :] - fs[h, 0:12, :]) / fs[h, 12:24, :]
        for k in range(NC):
            scale = []
            for i in range(RC // 128):
                h, r = divmod(k * (RC // 128) + i, 12)
                scale.append(scl[h, r:r + 1, :])
            p = eT[:, k * RC:(k + 1) * RC] * jnp.concatenate(scale, axis=1)
            for i in range(RC // 128):
                cp_ = cp_ + p[:, i * 128:(i + 1) * 128]
            wT[:, k * RC:(k + 1) * RC] = p.astype(BF16)
    with jax.named_scope("sums"):
        ax = [(x, y), (x, y), (y, x), (y, x)]

        def peer(q, first, k):
            ix, iy = x, y
            if (q < 2) == first:
                ix = (x + k) % 4
            else:
                iy = (y + k) % 4
            return iy * 4 + ix, (ix if (q < 2) == first else iy)

        c1 = [[] for _ in range(4)]
        for q in (0, 2, 1, 3):
            sums[q] = jnp.dot(wT[...], emb[:, q * 256:(q + 1) * 256], preferred_element_type=F32)
        for q in (0, 2, 1, 3):
            for k in range(1, 4):
                dev, pa = peer(q, True, k)
                cp = rcopy(sums.at[q, pl.ds(pl.multiple_of(pa * 64, 64), 64), :], r1.at[q, k - 1],
                           xs.at[0, q, k], xr.at[0, q, k], dp=dev)
                cp.start()
                c1[q].append(cp)
    with jax.named_scope("counts"):
        cg[dp] = jnp.broadcast_to(jnp.sum(jnp.transpose(cp_), axis=0, keepdims=True), (8, 256))
        nc = []
        for k in range(1, 16):
            cp = rcopy(cg.at[dp], cg.at[dp], ns.at[k], nr.at[k], dp=(dp + k) % 16)
            cp.start()
            nc.append(cp)

    with jax.named_scope("tabwait"):
        pc = []
        for j in range(16):
            if j:
                tc[j - 1].wait()
            dd = (dp + 16 - j) % 16
            cp = rcopy(tb.at[:, c, dd], tb.at[:, c, dd], ps.at[j], pr.at[j], sub=z * 2 + (1 - c))
            cp.start()
            pc.append(cp)
    with jax.named_scope("swap"):
        for cp in pc:
            cp.wait()
        la.wait()
    with jax.named_scope("widen"):
        for i in range(16):
            tf[pl.ds(i * 256, 256), :] = tb[i // 2, i % 2].reshape(256, 128).astype(F32)
    with jax.named_scope("gather"):
        def fetch(i, _):
            o = pl.multiple_of(i * 32, 32)
            for j in range(32):
                xg[pl.ds(o + j, 1), :] = tf[pl.ds(asg[o + j], 1), :]
            return 0
        lax.fori_loop(0, R // 32, fetch, 0)

    with jax.named_scope("stage1"):
        c2 = [[] for _ in range(4)]
        for q in (0, 2, 1, 3):
            for cp in c1[q]:
                cp.wait()
            a, b = ax[q]
            s1[q] = sums[q, pl.ds(pl.multiple_of(a * 64, 64), 64), :] + r1[q, 0] + r1[q, 1] + r1[q, 2]
            for k in range(1, 4):
                dev, pb = peer(q, False, k)
                cp = rcopy(s1.at[q, pl.ds(pl.multiple_of(pb * 16, 16), 16), :], r2.at[q, k - 1],
                           xs.at[1, q, k], xr.at[1, q, k], dp=dev)
                cp.start()
                c2[q].append(cp)

    with jax.named_scope("turn2"):
        mine = (lax.broadcasted_iota(jnp.int32, (RC, 128), 1) // 64) == c
        for k in range(NC):
            g = xg[pl.ds(k * RC, RC), :]
            cenT[:, pl.ds(k * RC, RC)] = jnp.transpose(g).astype(BF16)
            xgb[pl.ds(k * RC, RC), :] = jnp.where(mine, g, 1.0).astype(BF16)

    one = jnp.ones((16, RC), BF16)

    def code_logits(i):
        k, s = i // 4, i % 4
        cols = pl.ds(k * RC, RC)
        f = pl.ds(pl.multiple_of(c * 64 + 16 * s, 16), 16)
        es, cs_ = embT[f, cols], cenT[f, cols]
        xt = jnp.concatenate([es, es, es, cs_, cs_, cs_, one, one], axis=0)
        lsc[i % 2] = jnp.dot(cbt[s], xt, preferred_element_type=F32)

    def code(lo_, hi_):
        for i in range(lo_, hi_):
            k, s = i // 4, i % 4
            if i + 1 < 4 * NC:
                code_logits(i + 1)
            for j in range(RC // 256):
                l = lsc[i % 2, :, j * 256:(j + 1) * 256]
                e = jnp.exp2(l - jnp.max(l, axis=0, keepdims=True))
                w = e * (1.0 / jnp.sum(e, axis=0, keepdims=True))
                hi = w.astype(BF16)
                wh[s, :, j * 256:(j + 1) * 256] = hi
                wh[s, :, RC + j * 256:RC + (j + 1) * 256] = (w - hi.astype(F32)).astype(BF16)
            rows = pl.ds(k * RC, RC)
            both = jnp.concatenate([emb[rows, lanes128], xgb[rows, :]], axis=1)
            acc[s] += (jnp.dot(wh[s, :, 0:RC], both, preferred_element_type=F32)
                       + jnp.dot(wh[s, :, RC:2 * RC], both, preferred_element_type=F32))

    with jax.named_scope("code1"):
        code_logits(0)
        code(0, 12)

    with jax.named_scope("cntwait"):
        for cp in nc:
            cp.wait()
        ctot = jnp.sum(cg[...], axis=0)[0:1]
        cc[...] = jnp.transpose(jnp.broadcast_to(ctot, (128, 256))) + 1.0
    with jax.named_scope("stage2"):
        c3 = [[] for _ in range(4)]
        for q in (0, 2, 1, 3):
            for cp in c2[q]:
                cp.wait()
            a, b = ax[q]
            row = pl.ds(pl.multiple_of(a * 64 + b * 16, 16), 16)
            qs = slice(q * 256, (q + 1) * 256)
            fin = s1[q, pl.ds(pl.multiple_of(b * 16, 16), 16), :] + r2[q, 0] + r2[q, 1] + r2[q, 2]
            den = cc[row, :]
            out_ref[row, qs] = (fin + cent[row, qs].astype(F32)) / jnp.concatenate([den, den], axis=1)
            for k in range(1, 4):
                dev, _ = peer(q, False, k)
                piece = out_ref.at[row, pl.ds(q * 256, 256)]
                cp = rcopy(piece, piece, xs.at[2, q, k], xr.at[2, q, k], dp=dev)
                cp.start()
                c3[q].append(cp)

    with jax.named_scope("code2"):
        code(12, 4 * NC)

    with jax.named_scope("codeprep"):
        for s in range(4):
            accT[...] = jnp.transpose(acc[s])
            f = pl.multiple_of(c * 64 + s * 16, 16)
            tot16 = accT[pl.ds(f, 16), :] - accT[pl.ds(pl.multiple_of(128 + f, 16), 16), :]
            cnt = accT[pl.ds(pl.multiple_of(128 + (1 - c) * 64, 64), 8), :]
            for h in range(2):
                for g in range(2):
                    cs[s * 4 + h * 2 + g, 0:8, :] = tot16[8 * g:8 * g + 8, 128 * h:128 * h + 128]
                    cs[s * 4 + h * 2 + g, 8:16, :] = cnt[:, 128 * h:128 * h + 128]
    with jax.named_scope("codesend"):
        kc = []
        for k in range(1, 16):
            o = (dp + k) % 16
            cp = rcopy(cs.at[o], cr.at[dp], ks.at[k], kr.at[k], dp=o)
            cp.start()
            kc.append(cp)
        cr[dp] = cs[dp]
    with jax.named_scope("stage3"):
        c4 = []
        for q in (0, 2, 1, 3):
            for cp in c3[q]:
                cp.wait()
            a, b = ax[q]
            for k in range(1, 4):
                dev, _ = peer(q, True, k)
                piece = out_ref.at[pl.ds(pl.multiple_of(a * 64, 64), 64), pl.ds(q * 256, 256)]
                cp = rcopy(piece, piece, xs.at[3, q, k], xr.at[3, q, k], dp=dev)
                cp.start()
                c4.append(cp)

    with jax.named_scope("codewait"):
        for cp in kc:
            cp.wait()
    with jax.named_scope("codefin"):
        t = jnp.sum(cr[...], axis=0)
        so, ho, go = dp // 4, (dp // 2) % 2, dp % 2
        g8 = pl.ds(pl.multiple_of(go * 8, 8), 8)
        h128 = pl.ds(pl.multiple_of(ho * 128, 128), 128)
        cbo_ref[so, g8, h128] = (t[0:8] + cb[so, g8, h128]) / (t[8:16] + 1.0)
        oc = []
        for k in range(1, 16):
            piece = cbo_ref.at[so, g8, h128]
            cp = rcopy(piece, piece, os.at[k], orr.at[k], dp=(dp + k) % 16)
            cp.start()
            oc.append(cp)
    with jax.named_scope("newcent"):
        for cp in c4:
            cp.wait()
    with jax.named_scope("newcode"):
        for cp in oc:
            cp.wait()


def shards(embeddings, assignment, centroids, codebooks):
    dma = pltpu.SemaphoreType.DMA
    v = pltpu.VMEM
    hbm = pl.BlockSpec(memory_space=pltpu.HBM)
    vm = pl.BlockSpec(memory_space=pltpu.VMEM)
    return pl.pallas_call(
        kernel,
        out_shape=(v((KL, D), F32), v((4, 16, 256), F32)),
        in_specs=[hbm] * 4,
        out_specs=(vm, vm),
        scratch_shapes=[
            v((R, D), BF16), pltpu.SMEM((R,), jnp.int32), v((KL, D), BF16), v((4, 16, 256), F32),
            v((KL, R), F32), v((KL, R), BF16),
            v((2, 24, 128), F32), v((24, 128), F32), v((8, 24, 128), F32), v((2, 24, 128), F32), v((2, 12, 128), F32),
            v((8, 16, 128), BF16), v((8, 2, 16, 16, 128), BF16), v((4096, 128), F32), v((R, 128), F32),
            v((128, R), BF16), v((128, R), BF16), v((4, 256, 128), BF16),
            v((4, 256, 256), F32), v((4, 3, 64, 256), F32), v((4, 64, 256), F32), v((4, 3, 16, 256), F32),
            v((16, 8, 256), F32), v((256, 128), F32), v((4, 256, 256), F32), v((256, 256), F32),
            v((16, 16, 128), F32), v((16, 16, 128), F32),
            v((R, 128), BF16), v((2, 256, RC), F32), v((4, 256, 2 * RC), BF16),
            dma((9,)), dma((8,)), dma((8,)), dma((16,)), dma((16,)), dma((16,)), dma((16,)),
            dma((16,)), dma((16,)), dma((16,)), dma((16,)), dma((16,)), dma((16,)),
            dma((4, 4, 4)), dma((4, 4, 4)), dma((16,)), dma((16,)), dma((16,)), dma((16,)),
        ],
        compiler_params=pltpu.CompilerParams(
            collective_id=0, has_side_effects=True, vmem_limit_bytes=60 * 1024 * 1024),
        name="step",
    )(*(pltpu.with_memory_space_constraint(a, pltpu.HBM) for a in (embeddings, assignment, centroids, codebooks)))


def solution(mesh):
    placed = (P("dp", None), P("dp"), P("sub", None), P("sub", None, None))
    return jax.shard_map(
        shards,
        mesh=mesh,
        in_specs=placed,
        out_specs=(P("sub", None), P("sub", None, None)),
        check_vma=False,
    )
```

time: 165 us -> 54.6 us (0.33)
  Pallas kernels: 0 us -> 52.2 us
  waiting for transfers between devices: 51.4 us -> 0 us
  starting transfers between devices: 35.9 us -> 0 us
  matrix products: 35.4 us -> 0 us
  local copies, waits for them, and re-layouts: 22.2 us -> 1.6 us
  other arithmetic: 18.1 us -> 0 us
    pallas_call x0 -> x1, Pallas kernels: none -> 52.2 us  [shards(): pl.pallas_call(kernel, out_shape=(v((KL, D), F32), v((4, 16, 256), F32)),...]
    all_to_all x6 -> x0, waiting for transfers between devices: 51.4 us -> none  [the longest x3 39.8 us: from_everyone(): lax.all_to_all(jnp.broadcast_to(x[None], (length, *x.shape)), axis, 0, 0,...]
    all_to_all x6 -> x0, starting transfers between devices: 35.9 us -> none  [the longest x3 18.4 us: from_everyone(): lax.all_to_all(jnp.broadcast_to(x[None], (length, *x.shape)), axis, 0, 0,...]
    dot_general x4 -> x0, matrix products: 35.4 us -> none  [the longest x1 14.6 us: shards(): jnp.einsum('rsc,rsd->sdc', code_weights, res_parts, precision=lax.Precisi...]
    reduce_sum x9 -> x0, other arithmetic: 10.3 us -> none  [the longest x1 3.48 us: shards(): code_counts = jnp.sum(code_weights, axis=0)]
    gather x1 -> x0, local copies, waits for them, and re-layouts: 9.16 us -> none  [shards(): base_rows = jnp.take(cent_columns, assignment, axis=0).astype(jnp.float32)]
    broadcast_in_dim x3 -> x0, local copies, waits for them, and re-layouts: 3.5 us -> none  [from_everyone(): jnp.broadcast_to(x[None], (length, *x.shape))]
    unnamed x16 -> x2, local copies, waits for them, and re-layouts: 4.74 us -> 1.6 us
  transfers between devices with their start and end apart: 6 -> 0, of which waited for: 5 -> 0; matrix products, arithmetic and copies ran while one was open for 38% -> 0% of each run, Pallas kernels for 0% -> 0%
where the time goes in v2:
time: 54.6 us; the launch traced here: 54.5 us
  Pallas kernels  52.2 us (96%)
  local copies, waits for them, and re-layouts  1.6 us (3%)
  between operations  0.64 us (1%)
    pallas_call x1, Pallas kernels, shards(): pl.pallas_call(kernel, out_shape=(v((KL, D), F32), v((4, 16, 256), F32)),...  52.2 us
    unnamed x2, local copies, waits for them, and re-layouts  1.6 us

profile of v2, /device:TPU:1, one launch (start us, length us, event | category | flops | bytes accessed | tf_op | source)
XLA Modules:
  0.0 54.5 jit_solution(5007850882189189973)
XLA Ops:
  0.6 52.2 %step.1 = (f32[256,1024]{1,0:T(8,128)S(1)}, f32[4,16,256]{2,1,0:T(8,128)S(1)}) custom-call(bf16[3072,1024]{1,0:T(8,128)(2,1)} %emb_hbm.1, s32[3072]{0:T(1024)} %asg_hbm.1, bf16[256,1024]{1,0:T(8,128)(2,1)} %cent_hbm.1, f32[4,16,256]{2,1,0:T(8,128)} %cb_hbm.1), custom_call_target="tpu_custom_call" | custom-call | tf_op jit(solution)/shard_map/step/pallas_call | solution.py:342
  52.9 1.0 %copy.8 = f32[256,1024]{1,0:T(8,128)} copy(f32[256,1024]{1,0:T(8,128)S(1)} %get-tuple-element.2) | data formatting | bytes 2097152
  53.8 0.6 %copy.9 = f32[4,16,256]{2,1,0:T(8,128)} copy(f32[4,16,256]{2,1,0:T(8,128)S(1)} %get-tuple-element.3) | data formatting | bytes 131072

commit v3 on v2

v3 whole, which is shorter than its diff:
```python
import jax
import jax.numpy as jnp
from jax import lax
from jax.experimental import pallas as pl
from jax.experimental.pallas import tpu as pltpu
from jax.sharding import PartitionSpec as P

R, D, KL = 3072, 1024, 256
NC, RC = 6, 512
PAIR, BACK, ZFAR, ZNEAR, TAB, SWAP, SWAP2, OVERZ, COUNT, CODE, NEWCODE, CENT = range(12)
PHASES = CENT + 8
F32, BF16 = jnp.float32, jnp.bfloat16
LOG2E = 1.4426950408889634


def rcopy(src, dst, ssem, rsem, **where):
    return pltpu.make_async_remote_copy(
        src_ref=src, dst_ref=dst, send_sem=ssem, recv_sem=rsem,
        device_id=where, device_id_type=pl.DeviceIdType.MESH,
    )


def drain(ref, sem):
    pltpu.make_async_copy(ref, ref, sem).wait()


def split3(v):
    a = v.astype(BF16).astype(F32)
    r = v - a
    b = r.astype(BF16).astype(F32)
    return a, b, (r - b).astype(BF16).astype(F32)


def kernel(
    emb_hbm, asg_hbm, cent_hbm, cb_hbm, out_ref, cbo_ref,
    emb, asg, cent, cb, eT, wT, st, ra, mz, fs, scl, zbuf, tb, tf, xg, embT, cenT, cbt,
    sums, r1, s1, r2, cg, cc, acc, accT, cs, cr, xgb, lsc, wh,
    lsem, snd, rcv,
):
    dp = lax.axis_index("dp")
    sub = lax.axis_index("sub")
    y, x = dp // 4, dp % 4
    z, c = sub // 2, sub % 2

    def send(phase, src, dst, **where):
        rcopy(src, dst, snd.at[phase], rcv.at[phase], **where).start()

    with jax.named_scope("load"):
        lc = pltpu.make_async_copy(cent_hbm, cent, lsem.at[3])
        lb = pltpu.make_async_copy(cb_hbm, cb, lsem.at[4])
        la = pltpu.make_async_copy(asg_hbm, asg, lsem.at[5])
        lc.start()
        loads = []
        for k in range(3):
            sl = pl.ds(k * 1024, 1024)
            cp = pltpu.make_async_copy(emb_hbm.at[sl, :], emb.at[sl, :], lsem.at[k])
            cp.start()
            loads.append(cp)
        lb.start()
        la.start()
        bar = pltpu.get_barrier_semaphore()
        for k in range(1, 16):
            pl.semaphore_signal(bar, inc=1, device_id={"sub": (sub + k) % 16}, device_id_type=pl.DeviceIdType.MESH)
            pl.semaphore_signal(bar, inc=1, device_id={"dp": (dp + k) % 16}, device_id_type=pl.DeviceIdType.MESH)
        acc[...] = jnp.zeros(acc.shape, F32)
        rows16 = pl.ds(pl.multiple_of(dp * 16, 16), 16)
        lanes128 = pl.ds(pl.multiple_of(z * 128, 128), 128)
        lc.wait()
        tb[0, c] = cent[:, lanes128]

    with jax.named_scope("logits"):
        cf = cent[...].astype(F32)
        hn = 0.5 * jnp.sum(cf * cf, axis=1, keepdims=True)
        for k in range(NC):
            if k % 2 == 0:
                loads[k // 2].wait()
            l = lax.dot_general(cent[...], emb[k * RC:(k + 1) * RC, :], (((1,), (1,)), ((), ())),
                                preferred_element_type=F32) - hn
            m = jnp.max(l, axis=0, keepdims=True)
            e = jnp.exp(l - m)
            s = jnp.sum(e, axis=0, keepdims=True)
            eT[:, k * RC:(k + 1) * RC] = e
            for i in range(RC // 128):
                h, r = divmod(k * (RC // 128) + i, 12)
                st[h, r:r + 1, :] = m[:, i * 128:(i + 1) * 128]
                st[h, 12 + r:13 + r, :] = s[:, i * 128:(i + 1) * 128]

    with jax.named_scope("barrier"):
        pl.semaphore_wait(bar, 30)
    with jax.named_scope("statsend"):
        other = z * 2 + (1 - c)
        send(PAIR, st.at[1 - c], ra, sub=other)
    with jax.named_scope("zsend"):
        for k in range(3, 6):
            zz = (z + k) % 8
            send(ZFAR, cent.at[rows16, pl.ds(pl.multiple_of(zz * 128, 128), 128)], zbuf.at[5 - k], sub=zz * 2 + c)
    with jax.named_scope("cbprep"):
        lb.wait()
        for s in range(4):
            v = cb[s]
            parts = split3(v * LOG2E)
            half = split3(-0.5 * LOG2E * jnp.sum(v * v, axis=0, keepdims=True))
            neg = tuple(-p for p in parts)
            stack = jnp.concatenate(parts + neg + half + (jnp.zeros((29, 256), F32),), axis=0)
            cbt[s] = jnp.transpose(stack).astype(BF16)
        for k in range(NC):
            o = k * RC
            embT[:, pl.ds(o, RC)] = jnp.transpose(emb[pl.ds(o, RC), lanes128].astype(F32)).astype(BF16)

    with jax.named_scope("statwait"):
        drain(ra, rcv.at[PAIR])
    with jax.named_scope("merge"):
        ma, mb = st[c, 0:12, :], ra[0:12, :]
        big = jnp.maximum(ma, mb)
        mz[z, 0:12, :] = big
        mz[z, 12:24, :] = st[c, 12:24, :] * jnp.exp(ma - big) + ra[12:24, :] * jnp.exp(mb - big)
        for k in range(1, 8):
            send(OVERZ, mz.at[z], mz.at[z], sub=((z + k) % 8) * 2 + c)
        for k in (1, 7, 2, 6):
            zz = (z + k) % 8
            send(ZNEAR, cent.at[:, pl.ds(pl.multiple_of(zz * 128, 128), 128)], tb.at[8 - k, c], sub=zz * 2 + c)
    with jax.named_scope("zwait"):
        drain(zbuf, rcv.at[ZFAR])
    with jax.named_scope("tabsend"):
        tb[3:6, c, rows16] = zbuf[...]
        for j in range(1, 16):
            send(TAB, zbuf, tb.at[3:6, c, rows16], dp=(dp + j) % 16)
    with jax.named_scope("finwait"):
        drain(mz.at[0:7], rcv.at[OVERZ])
    with jax.named_scope("merge2"):
        mv = mz[:, 0:12, :]
        big = jnp.max(mv, axis=0)
        fs[c, 0:12, :] = big
        fs[c, 12:24, :] = jnp.sum(mz[:, 12:24, :] * jnp.exp(mv - big[None]), axis=0)
        send(BACK, fs.at[c], fs.at[c], sub=other)
        drain(ra, rcv.at[BACK])
    with jax.named_scope("weights"):
        cp_ = jnp.zeros((KL, 128), F32)
        for h in range(2):
            scl[h] = jnp.exp(st[h, 0:12, :] - fs[h, 0:12, :]) / fs[h, 12:24, :]
        for k in range(NC):
            scale = []
            for i in range(RC // 128):
                h, r = divmod(k * (RC // 128) + i, 12)
                scale.append(scl[h, r:r + 1, :])
            p = eT[:, k * RC:(k + 1) * RC] * jnp.concatenate(scale, axis=1)
            for i in range(RC // 128):
                cp_ = cp_ + p[:, i * 128:(i + 1) * 128]
            wT[:, k * RC:(k + 1) * RC] = p.astype(BF16)
    def along(i, first, k):
        if (i == 0) == first:
            return y * 4 + (x + k) % 4, (x + k) % 4
        return ((y + k) % 4) * 4 + x, (y + k) % 4

    ax = [(x, y), (y, x)]
    with jax.named_scope("sums"):
        for h in range(2):
            for q in (2 * h, 2 * h + 1):
                sums[q] = jnp.dot(wT[...], emb[:, q * 256:(q + 1) * 256], preferred_element_type=F32)
            for k in (1, 3, 2):
                for i in range(2):
                    dev, pa = along(i, True, k)
                    send(CENT + h, sums.at[2 * h + i, pl.ds(pl.multiple_of(pa * 64, 64), 64), :],
                         r1.at[h, i, k - 1], dp=dev)
    with jax.named_scope("counts"):
        cg[dp] = jnp.broadcast_to(jnp.sum(jnp.transpose(cp_), axis=0, keepdims=True), (8, 256))
        for k in range(1, 16):
            send(COUNT, cg.at[dp], cg.at[dp], dp=(dp + k) % 16)

    with jax.named_scope("nearwait"):
        drain(tb.at[0:4, 0], rcv.at[ZNEAR])
        send(SWAP, tb.at[0:3, c], tb.at[0:3, c], sub=other)
        send(SWAP, tb.at[6:8, c], tb.at[6:8, c], sub=other)
    with jax.named_scope("tabwait"):
        drain(tb.at[3:6, 0, 0:240], rcv.at[TAB])
        send(SWAP2, tb.at[3:6, c], tb.at[3:6, c], sub=other)
    with jax.named_scope("swap"):
        drain(tb.at[0:5, 0], rcv.at[SWAP])
        drain(tb.at[0:3, 0], rcv.at[SWAP2])
        la.wait()
    with jax.named_scope("widen"):
        for i in range(8):
            for j in range(2):
                at = pl.multiple_of(((z + i) % 8) * 512 + j * 256, 256)
                tf[pl.ds(at, 256), :] = tb[i, j].astype(F32)
    with jax.named_scope("gather"):
        def fetch(i, _):
            o = pl.multiple_of(i * 32, 32)
            for j in range(32):
                xg[pl.ds(o + j, 1), :] = tf[pl.ds(asg[o + j], 1), :]
            return 0
        lax.fori_loop(0, R // 32, fetch, 0)
    with jax.named_scope("turn"):
        mine = (lax.broadcasted_iota(jnp.int32, (RC, 128), 1) // 64) == c
        for k in range(NC):
            g = xg[pl.ds(k * RC, RC), :]
            cenT[:, pl.ds(k * RC, RC)] = jnp.transpose(g).astype(BF16)
            xgb[pl.ds(k * RC, RC), :] = jnp.where(mine, g, 1.0).astype(BF16)

    def stage1(h):
        drain(r1.at[h], rcv.at[CENT + h])
        for i in range(2):
            q = 2 * h + i
            s1[q] = (sums[q, pl.ds(pl.multiple_of(ax[i][0] * 64, 64), 64), :]
                     + r1[h, i, 0] + r1[h, i, 1] + r1[h, i, 2])
        for k in (1, 3, 2):
            for i in range(2):
                dev, pb = along(i, False, k)
                send(CENT + 2 + h, s1.at[2 * h + i, pl.ds(pl.multiple_of(pb * 16, 16), 16), :],
                     r2.at[h, i, k - 1], dp=dev)

    def stage2(h):
        drain(r2.at[h], rcv.at[CENT + 2 + h])
        for i in range(2):
            q = 2 * h + i
            a, b = ax[i]
            row = pl.ds(pl.multiple_of(a * 64 + b * 16, 16), 16)
            qs = slice(q * 256, (q + 1) * 256)
            fin = s1[q, pl.ds(pl.multiple_of(b * 16, 16), 16), :] + r2[h, i, 0] + r2[h, i, 1] + r2[h, i, 2]
            den = cc[row, :]
            out_ref[row, qs] = (fin + cent[row, qs].astype(F32)) / jnp.concatenate([den, den], axis=1)
        for k in (1, 3, 2):
            for i in range(2):
                a, b = ax[i]
                piece = out_ref.at[pl.ds(pl.multiple_of(a * 64 + b * 16, 16), 16), pl.ds((2 * h + i) * 256, 256)]
                send(CENT + 4 + h, piece, piece, dp=along(i, False, k)[0])

    def stage3(h):
        drain(r2.at[h], rcv.at[CENT + 4 + h])
        for k in (1, 3, 2):
            for i in range(2):
                piece = out_ref.at[pl.ds(pl.multiple_of(ax[i][0] * 64, 64), 64), pl.ds((2 * h + i) * 256, 256)]
                send(CENT + 6 + h, piece, piece, dp=along(i, True, k)[0])

    one = jnp.ones((16, RC), BF16)

    def code_logits(i):
        k, s = i // 4, i % 4
        cols = pl.ds(k * RC, RC)
        f = pl.ds(pl.multiple_of(c * 64 + 16 * s, 16), 16)
        es, cs_ = embT[f, cols], cenT[f, cols]
        xt = jnp.concatenate([es, es, es, cs_, cs_, cs_, one, one], axis=0)
        lsc[i % 2] = jnp.dot(cbt[s], xt, preferred_element_type=F32)

    def code(lo_, hi_):
        for i in range(lo_, hi_):
            k, s = i // 4, i % 4
            if i + 1 < 4 * NC:
                code_logits(i + 1)
            for j in range(RC // 256):
                l = lsc[i % 2, :, j * 256:(j + 1) * 256]
                e = jnp.exp2(l - jnp.max(l, axis=0, keepdims=True))
                w = e * (1.0 / jnp.sum(e, axis=0, keepdims=True))
                hi = w.astype(BF16)
                wh[s, :, j * 256:(j + 1) * 256] = hi
                wh[s, :, RC + j * 256:RC + (j + 1) * 256] = (w - hi.astype(F32)).astype(BF16)
            rows = pl.ds(k * RC, RC)
            both = jnp.concatenate([emb[rows, lanes128], xgb[rows, :]], axis=1)
            acc[s] += (jnp.dot(wh[s, :, 0:RC], both, preferred_element_type=F32)
                       + jnp.dot(wh[s, :, RC:2 * RC], both, preferred_element_type=F32))

    with jax.named_scope("code1"):
        code_logits(0)
        code(0, 4)
    with jax.named_scope("s1A"):
        stage1(0)
    with jax.named_scope("code2"):
        code(4, 12)
    with jax.named_scope("s1B"):
        stage1(1)
    with jax.named_scope("code3"):
        code(12, 16)
    with jax.named_scope("cntwait"):
        drain(cg.at[0:15], rcv.at[COUNT])
        ctot = jnp.sum(cg[...], axis=0)[0:1]
        cc[...] = jnp.transpose(jnp.broadcast_to(ctot, (128, 256))) + 1.0
    with jax.named_scope("s2A"):
        stage2(0)
    with jax.named_scope("code4"):
        code(16, 4 * NC)
    with jax.named_scope("codeprep"):
        for s in range(4):
            accT[...] = jnp.transpose(acc[s])
            f = pl.multiple_of(c * 64 + s * 16, 16)
            tot16 = accT[pl.ds(f, 16), :] - accT[pl.ds(pl.multiple_of(128 + f, 16), 16), :]
            cnt = accT[pl.ds(pl.multiple_of(128 + (1 - c) * 64, 64), 8), :]
            for h in range(2):
                for g in range(2):
                    cs[s * 4 + h * 2 + g, 0:8, :] = tot16[8 * g:8 * g + 8, 128 * h:128 * h + 128]
                    cs[s * 4 + h * 2 + g, 8:16, :] = cnt[:, 128 * h:128 * h + 128]
        for k in range(1, 16):
            o = (dp + k) % 16
            send(CODE, cs.at[o], cr.at[dp], dp=o)
        cr[dp] = cs[dp]
    with jax.named_scope("s2B"):
        stage2(1)
    with jax.named_scope("s3A"):
        stage3(0)
    with jax.named_scope("s3B"):
        stage3(1)
    with jax.named_scope("codewait"):
        drain(cr.at[0:15], rcv.at[CODE])
    with jax.named_scope("codefin"):
        t = jnp.sum(cr[...], axis=0)
        so, ho, go = dp // 4, (dp // 2) % 2, dp % 2
        g8 = pl.ds(pl.multiple_of(go * 8, 8), 8)
        h128 = pl.ds(pl.multiple_of(ho * 128, 128), 128)
        cbo_ref[so, g8, h128] = (t[0:8] + cb[so, g8, h128]) / (t[8:16] + 1.0)
        for k in range(1, 16):
            piece = cbo_ref.at[so, g8, h128]
            send(NEWCODE, piece, piece, dp=(dp + k) % 16)
    with jax.named_scope("newcent"):
        drain(r1.at[0], rcv.at[CENT + 6])
        drain(r1.at[1], rcv.at[CENT + 7])
    with jax.named_scope("newcode"):
        drain(cr.at[0:15, 0:8], rcv.at[NEWCODE])
    with jax.named_scope("sent"):
        sizes = {
            PAIR: ra, BACK: ra, ZFAR: zbuf, ZNEAR: tb.at[0:4, 0], TAB: tb.at[3:6, 0, 0:240], SWAP: tb.at[0:5, 0],
            SWAP2: tb.at[0:3, 0], OVERZ: mz.at[0:7], COUNT: cg.at[0:15], CODE: cr.at[0:15], NEWCODE: cr.at[0:15, 0:8],
        }
        for h in range(2):
            sizes |= {CENT + h: r1.at[h], CENT + 2 + h: r2.at[h], CENT + 4 + h: r2.at[h], CENT + 6 + h: r1.at[h]}
        for phase, ref in sizes.items():
            drain(ref, snd.at[phase])


def shards(embeddings, assignment, centroids, codebooks):
    dma = pltpu.SemaphoreType.DMA
    v = pltpu.VMEM
    hbm = pl.BlockSpec(memory_space=pltpu.HBM)
    vm = pl.BlockSpec(memory_space=pltpu.VMEM)
    return pl.pallas_call(
        kernel,
        out_shape=(v((KL, D), F32), v((4, 16, 256), F32)),
        in_specs=[hbm] * 4,
        out_specs=(vm, vm),
        scratch_shapes=[
            v((R, D), BF16), pltpu.SMEM((R,), jnp.int32), v((KL, D), BF16), v((4, 16, 256), F32),
            v((KL, R), F32), v((KL, R), BF16),
            v((2, 24, 128), F32), v((24, 128), F32), v((8, 24, 128), F32), v((2, 24, 128), F32), v((2, 12, 128), F32),
            v((3, 16, 128), BF16), v((8, 2, 256, 128), BF16), v((4096, 128), F32), v((R, 128), F32),
            v((128, R), BF16), v((128, R), BF16), v((4, 256, 128), BF16),
            v((4, 256, 256), F32), v((2, 2, 3, 64, 256), F32), v((4, 64, 256), F32), v((2, 2, 3, 16, 256), F32),
            v((16, 8, 256), F32), v((256, 128), F32), v((4, 256, 256), F32), v((256, 256), F32),
            v((16, 16, 128), F32), v((16, 16, 128), F32),
            v((R, 128), BF16), v((2, 256, RC), F32), v((4, 256, 2 * RC), BF16),
            dma((6,)), dma((PHASES,)), dma((PHASES,)),
        ],
        compiler_params=pltpu.CompilerParams(
            collective_id=0, has_side_effects=True, vmem_limit_bytes=60 * 1024 * 1024),
        name="step",
    )(*(pltpu.with_memory_space_constraint(a, pltpu.HBM) for a in (embeddings, assignment, centroids, codebooks)))


def solution(mesh):
    placed = (P("dp", None), P("dp"), P("sub", None), P("sub", None, None))
    return jax.shard_map(
        shards,
        mesh=mesh,
        in_specs=placed,
        out_specs=(P("sub", None), P("sub", None, None)),
        check_vma=False,
    )
```

time: 54.6 us -> 48.4 us (0.89)
  Pallas kernels: 52.2 us -> 46.1 us
    pallas_call x1, Pallas kernels: 52.2 us -> 46.1 us  [shards(): pl.pallas_call(kernel, out_shape=(v((KL, D), F32), v((4, 16, 256), F32)),...]
where the time goes in v3:
time: 48.4 us
  Pallas kernels  46.1 us (95%)
  local copies, waits for them, and re-layouts  1.6 us (3%)
  between operations  0.64 us (1%)
    pallas_call x1, Pallas kernels, shards(): pl.pallas_call(kernel, out_shape=(v((KL, D), F32), v((4, 16, 256), F32)),...  46.1 us
    unnamed x2, local copies, waits for them, and re-layouts  1.6 us

profile of v3, /device:TPU:1, one launch (start us, length us, event | category | flops | bytes accessed | tf_op | source)
XLA Modules:
  0.0 48.4 jit_solution(549764757712460478)
XLA Ops:
  0.6 46.1 %step.1 = (f32[256,1024]{1,0:T(8,128)S(1)}, f32[4,16,256]{2,1,0:T(8,128)S(1)}) custom-call(bf16[3072,1024]{1,0:T(8,128)(2,1)} %emb_hbm.1, s32[3072]{0:T(1024)} %asg_hbm.1, bf16[256,1024]{1,0:T(8,128)(2,1)} %cent_hbm.1, f32[4,16,256]{2,1,0:T(8,128)} %cb_hbm.1), custom_call_target="tpu_custom_call" | custom-call | tf_op jit(solution)/shard_map/step/pallas_call | solution.py:333
  46.8 1.0 %copy.8 = f32[256,1024]{1,0:T(8,128)} copy(f32[256,1024]{1,0:T(8,128)S(1)} %get-tuple-element.2) | data formatting | bytes 2097152
  47.7 0.6 %copy.9 = f32[4,16,256]{2,1,0:T(8,128)} copy(f32[4,16,256]{2,1,0:T(8,128)S(1)} %get-tuple-element.3) | data formatting | bytes 131072

commit v4 on v3

--- a/solution.py
+++ b/solution.py
@@ -7,7 +7,7 @@
 
 R, D, KL = 3072, 1024, 256
 NC, RC = 6, 512
-PAIR, BACK, ZFAR, ZNEAR, TAB, SWAP, SWAP2, OVERZ, COUNT, CODE, NEWCODE, CENT = range(12)
+PAIR, BACK, ZFAR, ZNEAR, ZNEAR2, TAB, SWAP, SWAP2, SWAP3, BASE, OVERZ, COUNT, CODE, NEWCODE, CENT = range(15)
 PHASES = CENT + 8
 F32, BF16 = jnp.float32, jnp.bfloat16
 LOG2E = 1.4426950408889634
@@ -33,7 +33,7 @@
 
 def kernel(
     emb_hbm, asg_hbm, cent_hbm, cb_hbm, out_ref, cbo_ref,
-    emb, asg, cent, cb, eT, wT, st, ra, mz, fs, scl, zbuf, tb, tf, xg, embT, cenT, cbt,
+    emb, asg, cent, cb, eT, wT, ml, st, ra, mz, fs, scl, zbuf, tb, tf, xg, gb, embT, cenT, cbt,
     sums, r1, s1, r2, cg, cc, acc, accT, cs, cr, xgb, lsc, wh,
     lsem, snd, rcv,
 ):
@@ -63,12 +63,15 @@
             pl.semaphore_signal(bar, inc=1, device_id={"sub": (sub + k) % 16}, device_id_type=pl.DeviceIdType.MESH)
             pl.semaphore_signal(bar, inc=1, device_id={"dp": (dp + k) % 16}, device_id_type=pl.DeviceIdType.MESH)
         acc[...] = jnp.zeros(acc.shape, F32)
+        st[...] = jnp.zeros(st.shape, F32)
+        ml[...] = jnp.zeros(ml.shape, F32)
         rows16 = pl.ds(pl.multiple_of(dp * 16, 16), 16)
         lanes128 = pl.ds(pl.multiple_of(z * 128, 128), 128)
         lc.wait()
         tb[0, c] = cent[:, lanes128]
 
     with jax.named_scope("logits"):
+        pad_one = jnp.where(lax.broadcasted_iota(jnp.int32, (2, 16, 128), 1) < 12, 0.0, 1.0)
         cf = cent[...].astype(F32)
         hn = 0.5 * jnp.sum(cf * cf, axis=1, keepdims=True)
         for k in range(NC):
@@ -82,8 +85,9 @@
             eT[:, k * RC:(k + 1) * RC] = e
             for i in range(RC // 128):
                 h, r = divmod(k * (RC // 128) + i, 12)
-                st[h, r:r + 1, :] = m[:, i * 128:(i + 1) * 128]
-                st[h, 12 + r:13 + r, :] = s[:, i * 128:(i + 1) * 128]
+                ml[h, r:r + 1, :] = m[:, i * 128:(i + 1) * 128]
+                st[h, r:r + 1, :] = s[:, i * 128:(i + 1) * 128]
+        st[...] = ml[...] + jnp.log(st[...] + pad_one)
 
     with jax.named_scope("barrier"):
         pl.semaphore_wait(bar, 30)
@@ -110,15 +114,14 @@
     with jax.named_scope("statwait"):
         drain(ra, rcv.at[PAIR])
     with jax.named_scope("merge"):
-        ma, mb = st[c, 0:12, :], ra[0:12, :]
+        ma, mb = st[c], ra[...]
         big = jnp.maximum(ma, mb)
-        mz[z, 0:12, :] = big
-        mz[z, 12:24, :] = st[c, 12:24, :] * jnp.exp(ma - big) + ra[12:24, :] * jnp.exp(mb - big)
+        mz[z] = big + jnp.log(jnp.exp(ma - big) + jnp.exp(mb - big))
         for k in range(1, 8):
             send(OVERZ, mz.at[z], mz.at[z], sub=((z + k) % 8) * 2 + c)
         for k in (1, 7, 2, 6):
             zz = (z + k) % 8
-            send(ZNEAR, cent.at[:, pl.ds(pl.multiple_of(zz * 128, 128), 128)], tb.at[8 - k, c], sub=zz * 2 + c)
+            send(ZNEAR if k in (1, 7) else ZNEAR2, cent.at[:, pl.ds(pl.multiple_of(zz * 128, 128), 128)], tb.at[8 - k, c], sub=zz * 2 + c)
     with jax.named_scope("zwait"):
         drain(zbuf, rcv.at[ZFAR])
     with jax.named_scope("tabsend"):
@@ -128,16 +131,18 @@
     with jax.named_scope("finwait"):
         drain(mz.at[0:7], rcv.at[OVERZ])
     with jax.named_scope("merge2"):
-        mv = mz[:, 0:12, :]
+        mv = mz[...]
         big = jnp.max(mv, axis=0)
-        fs[c, 0:12, :] = big
-        fs[c, 12:24, :] = jnp.sum(mz[:, 12:24, :] * jnp.exp(mv - big[None]), axis=0)
+        fs[c] = big + jnp.log(jnp.sum(jnp.exp(mv - big[None]), axis=0))
         send(BACK, fs.at[c], fs.at[c], sub=other)
+        drain(tb.at[0:2, 0], rcv.at[ZNEAR])
+        send(SWAP, tb.at[0:2, c], tb.at[0:2, c], sub=other)
+        send(SWAP, tb.at[7, c], tb.at[7, c], sub=other)
         drain(ra, rcv.at[BACK])
     with jax.named_scope("weights"):
         cp_ = jnp.zeros((KL, 128), F32)
         for h in range(2):
-            scl[h] = jnp.exp(st[h, 0:12, :] - fs[h, 0:12, :]) / fs[h, 12:24, :]
+            scl[h] = jnp.exp(ml[h] - fs[h])
         for k in range(NC):
             scale = []
             for i in range(RC // 128):
@@ -168,15 +173,16 @@
             send(COUNT, cg.at[dp], cg.at[dp], dp=(dp + k) % 16)
 
     with jax.named_scope("nearwait"):
-        drain(tb.at[0:4, 0], rcv.at[ZNEAR])
-        send(SWAP, tb.at[0:3, c], tb.at[0:3, c], sub=other)
-        send(SWAP, tb.at[6:8, c], tb.at[6:8, c], sub=other)
+        drain(tb.at[0:2, 0], rcv.at[ZNEAR2])
+        send(SWAP2, tb.at[2, c], tb.at[2, c], sub=other)
+        send(SWAP2, tb.at[6, c], tb.at[6, c], sub=other)
     with jax.named_scope("tabwait"):
         drain(tb.at[3:6, 0, 0:240], rcv.at[TAB])
-        send(SWAP2, tb.at[3:6, c], tb.at[3:6, c], sub=other)
+        send(SWAP3, tb.at[3:6, c], tb.at[3:6, c], sub=other)
     with jax.named_scope("swap"):
-        drain(tb.at[0:5, 0], rcv.at[SWAP])
-        drain(tb.at[0:3, 0], rcv.at[SWAP2])
+        drain(tb.at[0:3, 0], rcv.at[SWAP])
+        drain(tb.at[0:2, 0], rcv.at[SWAP2])
+        drain(tb.at[0:3, 0], rcv.at[SWAP3])
         la.wait()
     with jax.named_scope("widen"):
         for i in range(8):
@@ -187,15 +193,24 @@
         def fetch(i, _):
             o = pl.multiple_of(i * 32, 32)
             for j in range(32):
-                xg[pl.ds(o + j, 1), :] = tf[pl.ds(asg[o + j], 1), :]
+                xg[pl.ds(o + j, 1), :] = tf[pl.ds(asg[first + o + j], 1), :]
             return 0
-        lax.fori_loop(0, R // 32, fetch, 0)
-    with jax.named_scope("turn"):
-        mine = (lax.broadcasted_iota(jnp.int32, (RC, 128), 1) // 64) == c
-        for k in range(NC):
-            g = xg[pl.ds(k * RC, RC), :]
-            cenT[:, pl.ds(k * RC, RC)] = jnp.transpose(g).astype(BF16)
-            xgb[pl.ds(k * RC, RC), :] = jnp.where(mine, g, 1.0).astype(BF16)
+        first = c * (R // 2)
+        for k in range(3):
+            lax.fori_loop(k * 16, (k + 1) * 16, fetch, 0)
+            part = pl.ds(k * RC, RC)
+            gb[c, part, :] = xg[part, :].astype(BF16)
+            send(BASE, gb.at[c, part], gb.at[c, part], sub=other)
+
+    def block(k):
+        return pl.ds(pl.multiple_of(((c + k // 3) % 2 * 3 + k % 3) * RC, RC), RC)
+
+    mine = (lax.broadcasted_iota(jnp.int32, (RC, 128), 1) // 64) == c
+
+    def turn(k):
+        g = gb[(c + k // 3) % 2, pl.ds(k % 3 * RC, RC), :].astype(F32)
+        cenT[:, block(k)] = jnp.transpose(g).astype(BF16)
+        xgb[block(k), :] = jnp.where(mine, g, 1.0).astype(BF16)
 
     def stage1(h):
         drain(r1.at[h], rcv.at[CENT + h])
@@ -236,7 +251,7 @@
 
     def code_logits(i):
         k, s = i // 4, i % 4
-        cols = pl.ds(k * RC, RC)
+        cols = block(k)
         f = pl.ds(pl.multiple_of(c * 64 + 16 * s, 16), 16)
         es, cs_ = embT[f, cols], cenT[f, cols]
         xt = jnp.concatenate([es, es, es, cs_, cs_, cs_, one, one], axis=0)
@@ -254,22 +269,28 @@
                 hi = w.astype(BF16)
                 wh[s, :, j * 256:(j + 1) * 256] = hi
                 wh[s, :, RC + j * 256:RC + (j + 1) * 256] = (w - hi.astype(F32)).astype(BF16)
-            rows = pl.ds(k * RC, RC)
+            rows = block(k)
             both = jnp.concatenate([emb[rows, lanes128], xgb[rows, :]], axis=1)
             acc[s] += (jnp.dot(wh[s, :, 0:RC], both, preferred_element_type=F32)
                        + jnp.dot(wh[s, :, RC:2 * RC], both, preferred_element_type=F32))
 
     with jax.named_scope("code1"):
+        for k in range(3):
+            turn(k)
         code_logits(0)
-        code(0, 4)
+        code(0, 8)
     with jax.named_scope("s1A"):
         stage1(0)
     with jax.named_scope("code2"):
-        code(4, 12)
+        code(8, 11)
+        drain(gb.at[0], rcv.at[BASE])
+        for k in range(3, 6):
+            turn(k)
+        code(11, 16)
     with jax.named_scope("s1B"):
         stage1(1)
     with jax.named_scope("code3"):
-        code(12, 16)
+        code(16, 20)
     with jax.named_scope("cntwait"):
         drain(cg.at[0:15], rcv.at[COUNT])
         ctot = jnp.sum(cg[...], axis=0)[0:1]
@@ -277,7 +298,7 @@
     with jax.named_scope("s2A"):
         stage2(0)
     with jax.named_scope("code4"):
-        code(16, 4 * NC)
+        code(20, 4 * NC)
     with jax.named_scope("codeprep"):
         for s in range(4):
             accT[...] = jnp.transpose(acc[s])
@@ -316,8 +337,9 @@
         drain(cr.at[0:15, 0:8], rcv.at[NEWCODE])
     with jax.named_scope("sent"):
         sizes = {
-            PAIR: ra, BACK: ra, ZFAR: zbuf, ZNEAR: tb.at[0:4, 0], TAB: tb.at[3:6, 0, 0:240], SWAP: tb.at[0:5, 0],
-            SWAP2: tb.at[0:3, 0], OVERZ: mz.at[0:7], COUNT: cg.at[0:15], CODE: cr.at[0:15], NEWCODE: cr.at[0:15, 0:8],
+            PAIR: ra, BACK: ra, ZFAR: zbuf, ZNEAR: tb.at[0:2, 0], ZNEAR2: tb.at[0:2, 0],
+            TAB: tb.at[3:6, 0, 0:240], SWAP: tb.at[0:3, 0], SWAP2: tb.at[0:2, 0], SWAP3: tb.at[0:3, 0],
+            BASE: gb.at[0], OVERZ: mz.at[0:7], COUNT: cg.at[0:15], CODE: cr.at[0:15], NEWCODE: cr.at[0:15, 0:8],
         }
         for h in range(2):
             sizes |= {CENT + h: r1.at[h], CENT + 2 + h: r2.at[h], CENT + 4 + h: r2.at[h], CENT + 6 + h: r1.at[h]}
@@ -325,12 +347,21 @@
             drain(ref, snd.at[phase])
 
 
+def unload(cent_vm, code_vm, cent_out, code_out, sem):
+    a = pltpu.make_async_copy(cent_vm, cent_out, sem.at[0])
+    b = pltpu.make_async_copy(code_vm, code_out, sem.at[1])
+    a.start()
+    b.start()
+    a.wait()
+    b.wait()
+
+
 def shards(embeddings, assignment, centroids, codebooks):
     dma = pltpu.SemaphoreType.DMA
     v = pltpu.VMEM
     hbm = pl.BlockSpec(memory_space=pltpu.HBM)
     vm = pl.BlockSpec(memory_space=pltpu.VMEM)
-    return pl.pallas_call(
+    outs = pl.pallas_call(
         kernel,
         out_shape=(v((KL, D), F32), v((4, 16, 256), F32)),
         in_specs=[hbm] * 4,
@@ -338,8 +369,9 @@
         scratch_shapes=[
             v((R, D), BF16), pltpu.SMEM((R,), jnp.int32), v((KL, D), BF16), v((4, 16, 256), F32),
             v((KL, R), F32), v((KL, R), BF16),
-            v((2, 24, 128), F32), v((24, 128), F32), v((8, 24, 128), F32), v((2, 24, 128), F32), v((2, 12, 128), F32),
-            v((3, 16, 128), BF16), v((8, 2, 256, 128), BF16), v((4096, 128), F32), v((R, 128), F32),
+            v((2, 16, 128), F32), v((2, 16, 128), F32), v((16, 128), F32), v((8, 16, 128), F32), v((2, 16, 128), F32),
+            v((2, 16, 128), F32),
+            v((3, 16, 128), BF16), v((8, 2, 256, 128), BF16), v((4096, 128), F32), v((R // 2, 128), F32), v((2, R // 2, 128), BF16),
             v((128, R), BF16), v((128, R), BF16), v((4, 256, 128), BF16),
             v((4, 256, 256), F32), v((2, 2, 3, 64, 256), F32), v((4, 64, 256), F32), v((2, 2, 3, 16, 256), F32),
             v((16, 8, 256), F32), v((256, 128), F32), v((4, 256, 256), F32), v((256, 256), F32),
@@ -351,6 +383,15 @@
             collective_id=0, has_side_effects=True, vmem_limit_bytes=60 * 1024 * 1024),
         name="step",
     )(*(pltpu.with_memory_space_constraint(a, pltpu.HBM) for a in (embeddings, assignment, centroids, codebooks)))
+    hb = pltpu.HBM
+    return pl.pallas_call(
+        unload,
+        out_shape=(hb((KL, D), F32), hb((4, 16, 256), F32)),
+        in_specs=[vm] * 2,
+        out_specs=(hbm, hbm),
+        scratch_shapes=[dma((2,))],
+        name="unload",
+    )(*(pltpu.with_memory_space_constraint(a, pltpu.VMEM) for a in outs))
 
 
 def solution(mesh):

time: 48.4 us -> 46.8 us (0.967)
  local copies, waits for them, and re-layouts: 1.6 us -> 0 us
    unnamed x2 -> x0, local copies, waits for them, and re-layouts: 1.6 us -> none
    pallas_call x1, Pallas kernels: 46.1 us -> 44.9 us  [shards(): pl.pallas_call(kernel, out_shape=(v((KL, D), F32), v((4, 16, 256), F32)),...]
    pallas_call x0 -> x1, Pallas kernels: none -> 0.99 us  [shards(): pl.pallas_call(unload, out_shape=(hb((KL, D), F32), hb((4, 16, 256), F32)...]
where the time goes in v4:
time: 46.8 us; the launch traced here: 46.7 us
  Pallas kernels  45.9 us (98%)
  between operations  0.8 us (2%)
    pallas_call x1, Pallas kernels, shards(): pl.pallas_call(kernel, out_shape=(v((KL, D), F32), v((4, 16, 256), F32)),...  44.9 us
    pallas_call x1, Pallas kernels, shards(): pl.pallas_call(unload, out_shape=(hb((KL, D), F32), hb((4, 16, 256), F32)...  0.99 us

profile of v4, /device:TPU:1, one launch (start us, length us, event | category | flops | bytes accessed | tf_op | source)
XLA Modules:
  0.0 46.7 jit_solution(2511939659072045692)
XLA Ops:
  0.6 44.9 %step.1 = (f32[256,1024]{1,0:T(8,128)S(1)}, f32[4,16,256]{2,1,0:T(8,128)S(1)}) custom-call(bf16[3072,1024]{1,0:T(8,128)(2,1)} %emb_hbm.1, s32[3072]{0:T(1024)} %asg_hbm.1, bf16[256,1024]{1,0:T(8,128)(2,1)} %cent_hbm.1, f32[4,16,256]{2,1,0:T(8,128)} %cb_hbm.1), custom_call_target="tpu_custom_call" | custom-call | tf_op jit(solution)/shard_map/step/pallas_call | solution.py:364
  45.6 1.0 %unload.1 = (f32[256,1024]{1,0:T(8,128)}, f32[4,16,256]{2,1,0:T(8,128)}) custom-call(f32[256,1024]{1,0:T(8,128)S(1)} %get-tuple-element.4.cent_vm, f32[4,16,256]{2,1,0:T(8,128)S(1)} %get-tuple-element.5.code_vm), custom_call_target="tpu_custom_call" | custom-call | tf_op jit(solution)/shard_map/unload/pallas_call | solution.py:387

commit v5 on v4

--- a/solution.py
+++ b/solution.py
@@ -7,6 +7,7 @@
 
 R, D, KL = 3072, 1024, 256
 NC, RC = 6, 512
+LOADS = ((0, 512), (512, 1024), (1536, 1024), (2560, 512))
 PAIR, BACK, ZFAR, ZNEAR, ZNEAR2, TAB, SWAP, SWAP2, SWAP3, BASE, OVERZ, COUNT, CODE, NEWCODE, CENT = range(15)
 PHASES = CENT + 8
 F32, BF16 = jnp.float32, jnp.bfloat16
@@ -46,37 +47,34 @@
         rcopy(src, dst, snd.at[phase], rcv.at[phase], **where).start()
 
     with jax.named_scope("load"):
-        lc = pltpu.make_async_copy(cent_hbm, cent, lsem.at[3])
-        lb = pltpu.make_async_copy(cb_hbm, cb, lsem.at[4])
-        la = pltpu.make_async_copy(asg_hbm, asg, lsem.at[5])
+        lc = pltpu.make_async_copy(cent_hbm, cent, lsem.at[0])
+        lb = pltpu.make_async_copy(cb_hbm, cb, lsem.at[1])
+        la = pltpu.make_async_copy(asg_hbm, asg, lsem.at[2])
         lc.start()
-        loads = []
-        for k in range(3):
-            sl = pl.ds(k * 1024, 1024)
-            cp = pltpu.make_async_copy(emb_hbm.at[sl, :], emb.at[sl, :], lsem.at[k])
+        loads = {}
+        for k, (r0, n) in enumerate(LOADS):
+            cp = pltpu.make_async_copy(emb_hbm.at[r0:r0 + n, :], emb.at[r0:r0 + n, :], lsem.at[3 + k])
             cp.start()
-            loads.append(cp)
-        lb.start()
-        la.start()
+            loads[r0 // RC] = cp
         bar = pltpu.get_barrier_semaphore()
         for k in range(1, 16):
             pl.semaphore_signal(bar, inc=1, device_id={"sub": (sub + k) % 16}, device_id_type=pl.DeviceIdType.MESH)
             pl.semaphore_signal(bar, inc=1, device_id={"dp": (dp + k) % 16}, device_id_type=pl.DeviceIdType.MESH)
-        acc[...] = jnp.zeros(acc.shape, F32)
+        lb.start()
+        la.start()
         st[...] = jnp.zeros(st.shape, F32)
         ml[...] = jnp.zeros(ml.shape, F32)
         rows16 = pl.ds(pl.multiple_of(dp * 16, 16), 16)
         lanes128 = pl.ds(pl.multiple_of(z * 128, 128), 128)
-        lc.wait()
-        tb[0, c] = cent[:, lanes128]
 
     with jax.named_scope("logits"):
         pad_one = jnp.where(lax.broadcasted_iota(jnp.int32, (2, 16, 128), 1) < 12, 0.0, 1.0)
+        lc.wait()
         cf = cent[...].astype(F32)
         hn = 0.5 * jnp.sum(cf * cf, axis=1, keepdims=True)
         for k in range(NC):
-            if k % 2 == 0:
-                loads[k // 2].wait()
+            if k in loads:
+                loads[k].wait()
             l = lax.dot_general(cent[...], emb[k * RC:(k + 1) * RC, :], (((1,), (1,)), ((), ())),
                                 preferred_element_type=F32) - hn
             m = jnp.max(l, axis=0, keepdims=True)
@@ -99,6 +97,8 @@
             zz = (z + k) % 8
             send(ZFAR, cent.at[rows16, pl.ds(pl.multiple_of(zz * 128, 128), 128)], zbuf.at[5 - k], sub=zz * 2 + c)
     with jax.named_scope("cbprep"):
+        acc[...] = jnp.zeros(acc.shape, F32)
+        tb[0, c] = cent[:, lanes128]
         lb.wait()
         for s in range(4):
             v = cb[s]
@@ -168,9 +168,9 @@
                     send(CENT + h, sums.at[2 * h + i, pl.ds(pl.multiple_of(pa * 64, 64), 64), :],
                          r1.at[h, i, k - 1], dp=dev)
     with jax.named_scope("counts"):
-        cg[dp] = jnp.broadcast_to(jnp.sum(jnp.transpose(cp_), axis=0, keepdims=True), (8, 256))
+        cg[dp, 0:1, :] = jnp.sum(jnp.transpose(cp_), axis=0, keepdims=True)
         for k in range(1, 16):
-            send(COUNT, cg.at[dp], cg.at[dp], dp=(dp + k) % 16)
+            send(COUNT, cg.at[dp, 0:1], cg.at[dp, 0:1], dp=(dp + k) % 16)
 
     with jax.named_scope("nearwait"):
         drain(tb.at[0:2, 0], rcv.at[ZNEAR2])
@@ -191,13 +191,13 @@
                 tf[pl.ds(at, 256), :] = tb[i, j].astype(F32)
     with jax.named_scope("gather"):
         def fetch(i, _):
-            o = pl.multiple_of(i * 32, 32)
-            for j in range(32):
+            o = pl.multiple_of(i * 128, 128)
+            for j in range(128):
                 xg[pl.ds(o + j, 1), :] = tf[pl.ds(asg[first + o + j], 1), :]
             return 0
         first = c * (R // 2)
         for k in range(3):
-            lax.fori_loop(k * 16, (k + 1) * 16, fetch, 0)
+            lax.fori_loop(k * 4, (k + 1) * 4, fetch, 0)
             part = pl.ds(k * RC, RC)
             gb[c, part, :] = xg[part, :].astype(BF16)
             send(BASE, gb.at[c, part], gb.at[c, part], sub=other)
@@ -278,27 +278,33 @@
         for k in range(3):
             turn(k)
         code_logits(0)
-        code(0, 8)
+        code(0, 4)
     with jax.named_scope("s1A"):
         stage1(0)
     with jax.named_scope("code2"):
-        code(8, 11)
+        code(4, 11)
+    with jax.named_scope("basewait"):
         drain(gb.at[0], rcv.at[BASE])
+    with jax.named_scope("code3"):
         for k in range(3, 6):
             turn(k)
-        code(11, 16)
+        code(11, 12)
     with jax.named_scope("s1B"):
         stage1(1)
-    with jax.named_scope("code3"):
-        code(16, 20)
+    with jax.named_scope("code4"):
+        code(12, 16)
     with jax.named_scope("cntwait"):
-        drain(cg.at[0:15], rcv.at[COUNT])
-        ctot = jnp.sum(cg[...], axis=0)[0:1]
+        drain(cg.at[0:15, 0:1], rcv.at[COUNT])
+        ctot = jnp.sum(cg[:, 0:1, :], axis=0)
         cc[...] = jnp.transpose(jnp.broadcast_to(ctot, (128, 256))) + 1.0
     with jax.named_scope("s2A"):
         stage2(0)
-    with jax.named_scope("code4"):
-        code(20, 4 * NC)
+    with jax.named_scope("code5"):
+        code(16, 22)
+    with jax.named_scope("s2B"):
+        stage2(1)
+    with jax.named_scope("code6"):
+        code(22, 4 * NC)
     with jax.named_scope("codeprep"):
         for s in range(4):
             accT[...] = jnp.transpose(acc[s])
@@ -308,25 +314,24 @@
             for h in range(2):
                 for g in range(2):
                     cs[s * 4 + h * 2 + g, 0:8, :] = tot16[8 * g:8 * g + 8, 128 * h:128 * h + 128]
-                    cs[s * 4 + h * 2 + g, 8:16, :] = cnt[:, 128 * h:128 * h + 128]
+                    cs[s * 4 + h * 2 + g, 8:9, :] = cnt[0:1, 128 * h:128 * h + 128]
         for k in range(1, 16):
             o = (dp + k) % 16
-            send(CODE, cs.at[o], cr.at[dp], dp=o)
-        cr[dp] = cs[dp]
-    with jax.named_scope("s2B"):
-        stage2(1)
+            send(CODE, cs.at[o, 0:9], cr.at[dp, 0:9], dp=o)
+        cr[dp, 0:9, :] = cs[dp, 0:9, :]
     with jax.named_scope("s3A"):
         stage3(0)
     with jax.named_scope("s3B"):
         stage3(1)
     with jax.named_scope("codewait"):
-        drain(cr.at[0:15], rcv.at[CODE])
+        drain(cr.at[0:15, 0:9], rcv.at[CODE])
     with jax.named_scope("codefin"):
-        t = jnp.sum(cr[...], axis=0)
+        t = jnp.sum(cr[:, 0:8, :], axis=0)
+        n = jnp.sum(cr[:, 8:9, :], axis=0)
         so, ho, go = dp // 4, (dp // 2) % 2, dp % 2
         g8 = pl.ds(pl.multiple_of(go * 8, 8), 8)
         h128 = pl.ds(pl.multiple_of(ho * 128, 128), 128)
-        cbo_ref[so, g8, h128] = (t[0:8] + cb[so, g8, h128]) / (t[8:16] + 1.0)
+        cbo_ref[so, g8, h128] = (t + cb[so, g8, h128]) / (n + 1.0)
         for k in range(1, 16):
             piece = cbo_ref.at[so, g8, h128]
             send(NEWCODE, piece, piece, dp=(dp + k) % 16)
@@ -339,7 +344,7 @@
         sizes = {
             PAIR: ra, BACK: ra, ZFAR: zbuf, ZNEAR: tb.at[0:2, 0], ZNEAR2: tb.at[0:2, 0],
             TAB: tb.at[3:6, 0, 0:240], SWAP: tb.at[0:3, 0], SWAP2: tb.at[0:2, 0], SWAP3: tb.at[0:3, 0],
-            BASE: gb.at[0], OVERZ: mz.at[0:7], COUNT: cg.at[0:15], CODE: cr.at[0:15], NEWCODE: cr.at[0:15, 0:8],
+            BASE: gb.at[0], OVERZ: mz.at[0:7], COUNT: cg.at[0:15, 0:1], CODE: cr.at[0:15, 0:9], NEWCODE: cr.at[0:15, 0:8],
         }
         for h in range(2):
             sizes |= {CENT + h: r1.at[h], CENT + 2 + h: r2.at[h], CENT + 4 + h: r2.at[h], CENT + 6 + h: r1.at[h]}
@@ -377,7 +382,7 @@
             v((16, 8, 256), F32), v((256, 128), F32), v((4, 256, 256), F32), v((256, 256), F32),
             v((16, 16, 128), F32), v((16, 16, 128), F32),
             v((R, 128), BF16), v((2, 256, RC), F32), v((4, 256, 2 * RC), BF16),
-            dma((6,)), dma((PHASES,)), dma((PHASES,)),
+            dma((3 + len(LOADS),)), dma((PHASES,)), dma((PHASES,)),
         ],
         compiler_params=pltpu.CompilerParams(
             collective_id=0, has_side_effects=True, vmem_limit_bytes=60 * 1024 * 1024),

time: 46.8 us -> 45.5 us (0.972)
  Pallas kernels: 45.9 us -> 44.7 us
    pallas_call x1, Pallas kernels: 44.9 us -> 43.7 us  [shards(): pl.pallas_call(kernel, out_shape=(v((KL, D), F32), v((4, 16, 256), F32)),...]
where the time goes in v5:
time: 45.5 us
  Pallas kernels  44.7 us (98%)
  between operations  0.8 us (2%)
    pallas_call x1, Pallas kernels, shards(): pl.pallas_call(kernel, out_shape=(v((KL, D), F32), v((4, 16, 256), F32)),...  43.7 us
    pallas_call x1, Pallas kernels, shards(): pl.pallas_call(unload, out_shape=(hb((KL, D), F32), hb((4, 16, 256), F32)...  0.99 us

profile of v5, /device:TPU:1, one launch (start us, length us, event | category | flops | bytes accessed | tf_op | source)
XLA Modules:
  0.0 45.5 jit_solution(16688074841741938584)
XLA Ops:
  0.6 43.7 %step.1 = (f32[256,1024]{1,0:T(8,128)S(1)}, f32[4,16,256]{2,1,0:T(8,128)S(1)}) custom-call(bf16[3072,1024]{1,0:T(8,128)(2,1)} %emb_hbm.1, s32[3072]{0:T(1024)} %asg_hbm.1, bf16[256,1024]{1,0:T(8,128)(2,1)} %cent_hbm.1, f32[4,16,256]{2,1,0:T(8,128)} %cb_hbm.1), custom_call_target="tpu_custom_call" | custom-call | tf_op jit(solution)/shard_map/step/pallas_call | solution.py:369
  44.3 1.0 %unload.1 = (f32[256,1024]{1,0:T(8,128)}, f32[4,16,256]{2,1,0:T(8,128)}) custom-call(f32[256,1024]{1,0:T(8,128)S(1)} %get-tuple-element.4.cent_vm, f32[4,16,256]{2,1,0:T(8,128)S(1)} %get-tuple-element.5.code_vm), custom_call_target="tpu_custom_call" | custom-call | tf_op jit(solution)/shard_map/unload/pallas_call | solution.py:392

commit v6 on v5

--- a/solution.py
+++ b/solution.py
@@ -8,8 +8,9 @@
 R, D, KL = 3072, 1024, 256
 NC, RC = 6, 512
 LOADS = ((0, 512), (512, 1024), (1536, 1024), (2560, 512))
-PAIR, BACK, ZFAR, ZNEAR, ZNEAR2, TAB, SWAP, SWAP2, SWAP3, BASE, OVERZ, COUNT, CODE, NEWCODE, CENT = range(15)
-PHASES = CENT + 8
+PAIR, ZFAR, ZNEAR, TAB, SWAP, SWAP2, BASE, OVERZ, COUNT, CODE, NEWCODE, CENT = range(12)
+SCALE = CENT + 8
+PHASES = SCALE + 4
 F32, BF16 = jnp.float32, jnp.bfloat16
 LOG2E = 1.4426950408889634
 
@@ -34,8 +35,8 @@
 
 def kernel(
     emb_hbm, asg_hbm, cent_hbm, cb_hbm, out_ref, cbo_ref,
-    emb, asg, cent, cb, eT, wT, ml, st, ra, mz, fs, scl, zbuf, tb, tf, xg, gb, embT, cenT, cbt,
-    sums, r1, s1, r2, cg, cc, acc, accT, cs, cr, xgb, lsc, wh,
+    emb, asg, cent, cb, eT, wT, ml, st, ra, mz, scl, zbuf, tb, tf, xg, gb, embT, cenT, cbt,
+    sums, r1, s1, r2, cg, cc, acc, accT, cs, cr, xgb, lsc, wh, wb, scb,
     lsem, snd, rcv,
 ):
     dp = lax.axis_index("dp")
@@ -56,6 +57,7 @@
             cp = pltpu.make_async_copy(emb_hbm.at[r0:r0 + n, :], emb.at[r0:r0 + n, :], lsem.at[3 + k])
             cp.start()
             loads[r0 // RC] = cp
+        mz[...] = jnp.zeros(mz.shape, F32)
         bar = pltpu.get_barrier_semaphore()
         for k in range(1, 16):
             pl.semaphore_signal(bar, inc=1, device_id={"sub": (sub + k) % 16}, device_id_type=pl.DeviceIdType.MESH)
@@ -93,9 +95,9 @@
         other = z * 2 + (1 - c)
         send(PAIR, st.at[1 - c], ra, sub=other)
     with jax.named_scope("zsend"):
-        for k in range(3, 6):
+        for k in (4, 3, 5, 2, 6):
             zz = (z + k) % 8
-            send(ZFAR, cent.at[rows16, pl.ds(pl.multiple_of(zz * 128, 128), 128)], zbuf.at[5 - k], sub=zz * 2 + c)
+            send(ZFAR, cent.at[rows16, pl.ds(pl.multiple_of(zz * 128, 128), 128)], zbuf.at[6 - k], sub=zz * 2 + c)
     with jax.named_scope("cbprep"):
         acc[...] = jnp.zeros(acc.shape, F32)
         tb[0, c] = cent[:, lanes128]
@@ -116,33 +118,29 @@
     with jax.named_scope("merge"):
         ma, mb = st[c], ra[...]
         big = jnp.maximum(ma, mb)
-        mz[z] = big + jnp.log(jnp.exp(ma - big) + jnp.exp(mb - big))
-        for k in range(1, 8):
-            send(OVERZ, mz.at[z], mz.at[z], sub=((z + k) % 8) * 2 + c)
-        for k in (1, 7, 2, 6):
+        mz[c, z] = big + jnp.log(jnp.exp(ma - big) + jnp.exp(mb - big))
+        half = mz.at[c, z, 0:12]
+        for k in (4, 3, 5, 2, 6, 1, 7):
+            for core in range(2):
+                send(OVERZ, half, half, sub=((z + k) % 8) * 2 + core)
+        send(OVERZ, half, half, sub=other)
+        for k in (1, 7):
             zz = (z + k) % 8
-            send(ZNEAR if k in (1, 7) else ZNEAR2, cent.at[:, pl.ds(pl.multiple_of(zz * 128, 128), 128)], tb.at[8 - k, c], sub=zz * 2 + c)
+            send(ZNEAR, cent.at[:, pl.ds(pl.multiple_of(zz * 128, 128), 128)], tb.at[8 - k, c], sub=zz * 2 + c)
     with jax.named_scope("zwait"):
         drain(zbuf, rcv.at[ZFAR])
     with jax.named_scope("tabsend"):
-        tb[3:6, c, rows16] = zbuf[...]
+        tb[2:7, c, rows16] = zbuf[...]
         for j in range(1, 16):
-            send(TAB, zbuf, tb.at[3:6, c, rows16], dp=(dp + j) % 16)
+            send(TAB, zbuf, tb.at[2:7, c, rows16], dp=(dp + j) % 16)
     with jax.named_scope("finwait"):
-        drain(mz.at[0:7], rcv.at[OVERZ])
+        drain(cr.at[0:15, 0:12], rcv.at[OVERZ])
     with jax.named_scope("merge2"):
         mv = mz[...]
-        big = jnp.max(mv, axis=0)
-        fs[c] = big + jnp.log(jnp.sum(jnp.exp(mv - big[None]), axis=0))
-        send(BACK, fs.at[c], fs.at[c], sub=other)
-        drain(tb.at[0:2, 0], rcv.at[ZNEAR])
-        send(SWAP, tb.at[0:2, c], tb.at[0:2, c], sub=other)
-        send(SWAP, tb.at[7, c], tb.at[7, c], sub=other)
-        drain(ra, rcv.at[BACK])
+        big = jnp.max(mv, axis=1)
+        scl[...] = jnp.exp(ml[...] - (big + jnp.log(jnp.sum(jnp.exp(mv - big[:, None]), axis=1))))
     with jax.named_scope("weights"):
         cp_ = jnp.zeros((KL, 128), F32)
-        for h in range(2):
-            scl[h] = jnp.exp(ml[h] - fs[h])
         for k in range(NC):
             scale = []
             for i in range(RC // 128):
@@ -167,22 +165,21 @@
                     dev, pa = along(i, True, k)
                     send(CENT + h, sums.at[2 * h + i, pl.ds(pl.multiple_of(pa * 64, 64), 64), :],
                          r1.at[h, i, k - 1], dp=dev)
+            if h == 0:
+                drain(tb.at[0:2, 0], rcv.at[ZNEAR])
+                send(SWAP, tb.at[0:2, c], tb.at[0:2, c], sub=other)
+                send(SWAP, tb.at[7, c], tb.at[7, c], sub=other)
     with jax.named_scope("counts"):
         cg[dp, 0:1, :] = jnp.sum(jnp.transpose(cp_), axis=0, keepdims=True)
         for k in range(1, 16):
             send(COUNT, cg.at[dp, 0:1], cg.at[dp, 0:1], dp=(dp + k) % 16)
 
-    with jax.named_scope("nearwait"):
-        drain(tb.at[0:2, 0], rcv.at[ZNEAR2])
-        send(SWAP2, tb.at[2, c], tb.at[2, c], sub=other)
-        send(SWAP2, tb.at[6, c], tb.at[6, c], sub=other)
     with jax.named_scope("tabwait"):
-        drain(tb.at[3:6, 0, 0:240], rcv.at[TAB])
-        send(SWAP3, tb.at[3:6, c], tb.at[3:6, c], sub=other)
+        drain(tb.at[2:7, 0, 0:240], rcv.at[TAB])
+        send(SWAP2, tb.at[2:7, c], tb.at[2:7, c], sub=other)
     with jax.named_scope("swap"):
         drain(tb.at[0:3, 0], rcv.at[SWAP])
-        drain(tb.at[0:2, 0], rcv.at[SWAP2])
-        drain(tb.at[0:3, 0], rcv.at[SWAP3])
+        drain(tb.at[0:5, 0], rcv.at[SWAP2])
         la.wait()
     with jax.named_scope("widen"):
         for i in range(8):
@@ -212,6 +209,8 @@
         cenT[:, block(k)] = jnp.transpose(g).astype(BF16)
         xgb[block(k), :] = jnp.where(mine, g, 1.0).astype(BF16)
 
+    diag = (lax.broadcasted_iota(jnp.int32, (16, 128), 0) == lax.broadcasted_iota(jnp.int32, (16, 128), 1))
+
     def stage1(h):
         drain(r1.at[h], rcv.at[CENT + h])
         for i in range(2):
@@ -233,19 +232,44 @@
             qs = slice(q * 256, (q + 1) * 256)
             fin = s1[q, pl.ds(pl.multiple_of(b * 16, 16), 16), :] + r2[h, i, 0] + r2[h, i, 1] + r2[h, i, 2]
             den = cc[row, :]
-            out_ref[row, qs] = (fin + cent[row, qs].astype(F32)) / jnp.concatenate([den, den], axis=1)
+            v = (fin + cent[row, qs].astype(F32)) / jnp.concatenate([den, den], axis=1)
+            top = jnp.maximum(jnp.max(jnp.abs(v), axis=1, keepdims=True), 1e-30)
+            code_ = jnp.floor(v * (32767.0 / top) + 0.5).astype(jnp.int32)
+            wb[h, i, row, :] = (code_[:, 0:128] << 16) | (code_[:, 128:256] & 0xFFFF)
+            unit = jnp.broadcast_to(top * (1.0 / 32767.0), (16, 128))
+            scb[h, i, a * 4 + b, 0:1, :] = jnp.sum(jnp.where(diag, unit, 0.0), axis=0, keepdims=True)
         for k in (1, 3, 2):
             for i in range(2):
                 a, b = ax[i]
-                piece = out_ref.at[pl.ds(pl.multiple_of(a * 64 + b * 16, 16), 16), pl.ds((2 * h + i) * 256, 256)]
-                send(CENT + 4 + h, piece, piece, dp=along(i, False, k)[0])
+                dev = along(i, False, k)[0]
+                piece = wb.at[h, i, pl.ds(pl.multiple_of(a * 64 + b * 16, 16), 16)]
+                send(CENT + 4 + h, piece, piece, dp=dev)
+                piece = scb.at[h, i, a * 4 + b, 0:1]
+                send(SCALE + h, piece, piece, dp=dev)
 
     def stage3(h):
-        drain(r2.at[h], rcv.at[CENT + 4 + h])
+        drain(wb.at[h, 0, 0:96], rcv.at[CENT + 4 + h])
+        drain(scb.at[h, 0, 0:6, 0:1], rcv.at[SCALE + h])
         for k in (1, 3, 2):
             for i in range(2):
-                piece = out_ref.at[pl.ds(pl.multiple_of(ax[i][0] * 64, 64), 64), pl.ds((2 * h + i) * 256, 256)]
-                send(CENT + 6 + h, piece, piece, dp=along(i, True, k)[0])
+                dev = along(i, True, k)[0]
+                piece = wb.at[h, i, pl.ds(pl.multiple_of(ax[i][0] * 64, 64), 64)]
+                send(CENT + 6 + h, piece, piece, dp=dev)
+                piece = scb.at[h, i, pl.ds(ax[i][0] * 4, 4), 0:1]
+                send(SCALE + 2 + h, piece, piece, dp=dev)
+
+    def stage4(h):
+        drain(wb.at[h, :, 0:192], rcv.at[CENT + 6 + h])
+        drain(scb.at[h, :, 0:12, 0:1], rcv.at[SCALE + 2 + h])
+        for i in range(2):
+            q = (2 * h + i) * 256
+            for r in range(16):
+                rows = slice(r * 16, r * 16 + 16)
+                unit = jnp.sum(jnp.where(diag, jnp.broadcast_to(scb[h, i, r, 0:1, :], (16, 128)), 0.0),
+                               axis=1, keepdims=True)
+                w = wb[h, i, rows, :]
+                out_ref[rows, q:q + 128] = (w >> 16).astype(F32) * unit
+                out_ref[rows, q + 128:q + 256] = ((w << 16) >> 16).astype(F32) * unit
 
     one = jnp.ones((16, RC), BF16)
 
@@ -274,6 +298,16 @@
             acc[s] += (jnp.dot(wh[s, :, 0:RC], both, preferred_element_type=F32)
                        + jnp.dot(wh[s, :, RC:2 * RC], both, preferred_element_type=F32))
 
+    def prepare(s):
+        accT[s] = jnp.transpose(acc[s])
+        f = pl.multiple_of(c * 64 + s * 16, 16)
+        tot16 = accT[s, pl.ds(f, 16), :] - accT[s, pl.ds(pl.multiple_of(128 + f, 16), 16), :]
+        cnt = accT[s, pl.ds(pl.multiple_of(128 + (1 - c) * 64, 64), 8), :]
+        for h in range(2):
+            for g in range(2):
+                cs[s * 4 + h * 2 + g, 0:8, :] = tot16[8 * g:8 * g + 8, 128 * h:128 * h + 128]
+                cs[s * 4 + h * 2 + g, 8:9, :] = cnt[0:1, 128 * h:128 * h + 128]
+
     with jax.named_scope("code1"):
         for k in range(3):
             turn(k)
@@ -288,11 +322,11 @@
     with jax.named_scope("code3"):
         for k in range(3, 6):
             turn(k)
-        code(11, 12)
+        code(11, 13)
     with jax.named_scope("s1B"):
         stage1(1)
     with jax.named_scope("code4"):
-        code(12, 16)
+        code(13, 17)
     with jax.named_scope("cntwait"):
         drain(cg.at[0:15, 0:1], rcv.at[COUNT])
         ctot = jnp.sum(cg[:, 0:1, :], axis=0)
@@ -300,25 +334,18 @@
     with jax.named_scope("s2A"):
         stage2(0)
     with jax.named_scope("code5"):
-        code(16, 22)
-    with jax.named_scope("s2B"):
-        stage2(1)
-    with jax.named_scope("code6"):
-        code(22, 4 * NC)
+        code(17, 21)
+        for s in range(3):
+            prepare(s)
+            code(21 + s, 22 + s)
+        prepare(3)
     with jax.named_scope("codeprep"):
-        for s in range(4):
-            accT[...] = jnp.transpose(acc[s])
-            f = pl.multiple_of(c * 64 + s * 16, 16)
-            tot16 = accT[pl.ds(f, 16), :] - accT[pl.ds(pl.multiple_of(128 + f, 16), 16), :]
-            cnt = accT[pl.ds(pl.multiple_of(128 + (1 - c) * 64, 64), 8), :]
-            for h in range(2):
-                for g in range(2):
-                    cs[s * 4 + h * 2 + g, 0:8, :] = tot16[8 * g:8 * g + 8, 128 * h:128 * h + 128]
-                    cs[s * 4 + h * 2 + g, 8:9, :] = cnt[0:1, 128 * h:128 * h + 128]
         for k in range(1, 16):
             o = (dp + k) % 16
             send(CODE, cs.at[o, 0:9], cr.at[dp, 0:9], dp=o)
         cr[dp, 0:9, :] = cs[dp, 0:9, :]
+    with jax.named_scope("s2B"):
+        stage2(1)
     with jax.named_scope("s3A"):
         stage3(0)
     with jax.named_scope("s3B"):
@@ -336,29 +363,33 @@
             piece = cbo_ref.at[so, g8, h128]
             send(NEWCODE, piece, piece, dp=(dp + k) % 16)
     with jax.named_scope("newcent"):
-        drain(r1.at[0], rcv.at[CENT + 6])
-        drain(r1.at[1], rcv.at[CENT + 7])
+        stage4(0)
+        stage4(1)
     with jax.named_scope("newcode"):
         drain(cr.at[0:15, 0:8], rcv.at[NEWCODE])
     with jax.named_scope("sent"):
         sizes = {
-            PAIR: ra, BACK: ra, ZFAR: zbuf, ZNEAR: tb.at[0:2, 0], ZNEAR2: tb.at[0:2, 0],
-            TAB: tb.at[3:6, 0, 0:240], SWAP: tb.at[0:3, 0], SWAP2: tb.at[0:2, 0], SWAP3: tb.at[0:3, 0],
-            BASE: gb.at[0], OVERZ: mz.at[0:7], COUNT: cg.at[0:15, 0:1], CODE: cr.at[0:15, 0:9], NEWCODE: cr.at[0:15, 0:8],
+            PAIR: ra, ZFAR: zbuf, ZNEAR: tb.at[0:2, 0],
+            TAB: tb.at[2:7, 0, 0:240], SWAP: tb.at[0:3, 0], SWAP2: tb.at[0:5, 0],
+            BASE: gb.at[0], OVERZ: cr.at[0:15, 0:12], COUNT: cg.at[0:15, 0:1], CODE: cr.at[0:15, 0:9], NEWCODE: cr.at[0:15, 0:8],
         }
         for h in range(2):
-            sizes |= {CENT + h: r1.at[h], CENT + 2 + h: r2.at[h], CENT + 4 + h: r2.at[h], CENT + 6 + h: r1.at[h]}
+            sizes |= {CENT + h: r1.at[h], CENT + 2 + h: r2.at[h], CENT + 4 + h: wb.at[h, 0, 0:96],
+                      CENT + 6 + h: wb.at[h, :, 0:192], SCALE + h: scb.at[h, 0, 0:6, 0:1],
+                      SCALE + 2 + h: scb.at[h, :, 0:12, 0:1]}
         for phase, ref in sizes.items():
             drain(ref, snd.at[phase])
 
 
 def unload(cent_vm, code_vm, cent_out, code_out, sem):
-    a = pltpu.make_async_copy(cent_vm, cent_out, sem.at[0])
-    b = pltpu.make_async_copy(code_vm, code_out, sem.at[1])
-    a.start()
-    b.start()
-    a.wait()
-    b.wait()
+    copies = [pltpu.make_async_copy(code_vm, code_out, sem.at[4])]
+    for k in range(4):
+        rows = pl.ds(k * 64, 64)
+        copies.append(pltpu.make_async_copy(cent_vm.at[rows], cent_out.at[rows], sem.at[k]))
+    for cp in copies:
+        cp.start()
+    for cp in copies:
+        cp.wait()
 
 
 def shards(embeddings, assignment, centroids, codebooks):
@@ -374,14 +405,14 @@
         scratch_shapes=[
             v((R, D), BF16), pltpu.SMEM((R,), jnp.int32), v((KL, D), BF16), v((4, 16, 256), F32),
             v((KL, R), F32), v((KL, R), BF16),
-            v((2, 16, 128), F32), v((2, 16, 128), F32), v((16, 128), F32), v((8, 16, 128), F32), v((2, 16, 128), F32),
-            v((2, 16, 128), F32),
-            v((3, 16, 128), BF16), v((8, 2, 256, 128), BF16), v((4096, 128), F32), v((R // 2, 128), F32), v((2, R // 2, 128), BF16),
+            v((2, 16, 128), F32), v((2, 16, 128), F32), v((16, 128), F32), v((2, 8, 16, 128), F32), v((2, 16, 128), F32),
+            v((5, 16, 128), BF16), v((8, 2, 256, 128), BF16), v((4096, 128), F32), v((R // 2, 128), F32), v((2, R // 2, 128), BF16),
             v((128, R), BF16), v((128, R), BF16), v((4, 256, 128), BF16),
             v((4, 256, 256), F32), v((2, 2, 3, 64, 256), F32), v((4, 64, 256), F32), v((2, 2, 3, 16, 256), F32),
-            v((16, 8, 256), F32), v((256, 128), F32), v((4, 256, 256), F32), v((256, 256), F32),
+            v((16, 8, 256), F32), v((256, 128), F32), v((4, 256, 256), F32), v((4, 256, 256), F32),
             v((16, 16, 128), F32), v((16, 16, 128), F32),
             v((R, 128), BF16), v((2, 256, RC), F32), v((4, 256, 2 * RC), BF16),
+            v((2, 2, 256, 128), jnp.int32), v((2, 2, 16, 8, 128), F32),
             dma((3 + len(LOADS),)), dma((PHASES,)), dma((PHASES,)),
         ],
         compiler_params=pltpu.CompilerParams(
@@ -394,7 +425,7 @@
         out_shape=(hb((KL, D), F32), hb((4, 16, 256), F32)),
         in_specs=[vm] * 2,
         out_specs=(hbm, hbm),
-        scratch_shapes=[dma((2,))],
+        scratch_shapes=[dma((5,))],
         name="unload",
     )(*(pltpu.with_memory_space_constraint(a, pltpu.VMEM) for a in outs))
 

time: 45.5 us -> 45 us (0.989)
  Pallas kernels: 44.7 us -> 44.1 us
    pallas_call x1, Pallas kernels: 43.7 us -> 43.1 us  [shards(): pl.pallas_call(kernel, out_shape=(v((KL, D), F32), v((4, 16, 256), F32)),...]
where the time goes in v6:
time: 45 us; the launch traced here: 44.9 us
  Pallas kernels  44.1 us (98%)
  between operations  0.8 us (2%)
    pallas_call x1, Pallas kernels, shards(): pl.pallas_call(kernel, out_shape=(v((KL, D), F32), v((4, 16, 256), F32)),...  43.1 us
    pallas_call x1, Pallas kernels, shards(): pl.pallas_call(unload, out_shape=(hb((KL, D), F32), hb((4, 16, 256), F32)...  1.03 us

profile of v6, /device:TPU:1, one launch (start us, length us, event | category | flops | bytes accessed | tf_op | source)
XLA Modules:
  0.0 44.9 jit_solution(7205146425710281443)
XLA Ops:
  0.6 43.1 %step.1 = (f32[256,1024]{1,0:T(8,128)S(1)}, f32[4,16,256]{2,1,0:T(8,128)S(1)}) custom-call(bf16[3072,1024]{1,0:T(8,128)(2,1)} %emb_hbm.1, s32[3072]{0:T(1024)} %asg_hbm.1, bf16[256,1024]{1,0:T(8,128)(2,1)} %cent_hbm.1, f32[4,16,256]{2,1,0:T(8,128)} %cb_hbm.1), custom_call_target="tpu_custom_call" | custom-call | tf_op jit(solution)/shard_map/step/pallas_call | solution.py:400
  43.7 1.0 %unload.1 = (f32[256,1024]{1,0:T(8,128)}, f32[4,16,256]{2,1,0:T(8,128)}) custom-call(f32[256,1024]{1,0:T(8,128)S(1)} %get-tuple-element.4.cent_vm, f32[4,16,256]{2,1,0:T(8,128)S(1)} %get-tuple-element.5.code_vm), custom_call_target="tpu_custom_call" | custom-call | tf_op jit(solution)/shard_map/unload/pallas_call | solution.py:423

commit v7 on v6

--- a/solution.py
+++ b/solution.py
@@ -77,6 +77,12 @@
         for k in range(NC):
             if k in loads:
                 loads[k].wait()
+            if k == 3:
+                with jax.named_scope("barrier"):
+                    pl.semaphore_wait(bar, 30)
+                for d in (4, 3, 5, 2, 6):
+                    zz = (z + d) % 8
+                    send(ZFAR, cent.at[rows16, pl.ds(pl.multiple_of(zz * 128, 128), 128)], zbuf.at[6 - d], sub=zz * 2 + c)
             l = lax.dot_general(cent[...], emb[k * RC:(k + 1) * RC, :], (((1,), (1,)), ((), ())),
                                 preferred_element_type=F32) - hn
             m = jnp.max(l, axis=0, keepdims=True)
@@ -89,15 +95,9 @@
                 st[h, r:r + 1, :] = s[:, i * 128:(i + 1) * 128]
         st[...] = ml[...] + jnp.log(st[...] + pad_one)
 
-    with jax.named_scope("barrier"):
-        pl.semaphore_wait(bar, 30)
     with jax.named_scope("statsend"):
         other = z * 2 + (1 - c)
         send(PAIR, st.at[1 - c], ra, sub=other)
-    with jax.named_scope("zsend"):
-        for k in (4, 3, 5, 2, 6):
-            zz = (z + k) % 8
-            send(ZFAR, cent.at[rows16, pl.ds(pl.multiple_of(zz * 128, 128), 128)], zbuf.at[6 - k], sub=zz * 2 + c)
     with jax.named_scope("cbprep"):
         acc[...] = jnp.zeros(acc.shape, F32)
         tb[0, c] = cent[:, lanes128]

time: 45 us -> 43.3 us (0.962)
  Pallas kernels: 44.1 us -> 42.4 us
    pallas_call x1, Pallas kernels: 43.1 us -> 41.4 us  [shards(): pl.pallas_call(kernel, out_shape=(v((KL, D), F32), v((4, 16, 256), F32)),...]
where the time goes in v7:
time: 43.3 us; the launch traced here: 43.2 us
  Pallas kernels  42.4 us (98%)
  between operations  0.8 us (2%)
    pallas_call x1, Pallas kernels, shards(): pl.pallas_call(kernel, out_shape=(v((KL, D), F32), v((4, 16, 256), F32)),...  41.4 us
    pallas_call x1, Pallas kernels, shards(): pl.pallas_call(unload, out_shape=(hb((KL, D), F32), hb((4, 16, 256), F32)...  1.03 us

profile of v7, /device:TPU:1, one launch (start us, length us, event | category | flops | bytes accessed | tf_op | source)
XLA Modules:
  0.0 43.2 jit_solution(9858214222816390078)
XLA Ops:
  0.6 41.4 %step.1 = (f32[256,1024]{1,0:T(8,128)S(1)}, f32[4,16,256]{2,1,0:T(8,128)S(1)}) custom-call(bf16[3072,1024]{1,0:T(8,128)(2,1)} %emb_hbm.1, s32[3072]{0:T(1024)} %asg_hbm.1, bf16[256,1024]{1,0:T(8,128)(2,1)} %cent_hbm.1, f32[4,16,256]{2,1,0:T(8,128)} %cb_hbm.1), custom_call_target="tpu_custom_call" | custom-call | tf_op jit(solution)/shard_map/step/pallas_call | solution.py:400
  42.0 1.0 %unload.1 = (f32[256,1024]{1,0:T(8,128)}, f32[4,16,256]{2,1,0:T(8,128)}) custom-call(f32[256,1024]{1,0:T(8,128)S(1)} %get-tuple-element.4.cent_vm, f32[4,16,256]{2,1,0:T(8,128)S(1)} %get-tuple-element.5.code_vm), custom_call_target="tpu_custom_call" | custom-call | tf_op jit(solution)/shard_map/unload/pallas_call | solution.py:423

commit v8 on v7

--- a/solution.py
+++ b/solution.py
@@ -83,6 +83,9 @@
                 for d in (4, 3, 5, 2, 6):
                     zz = (z + d) % 8
                     send(ZFAR, cent.at[rows16, pl.ds(pl.multiple_of(zz * 128, 128), 128)], zbuf.at[6 - d], sub=zz * 2 + c)
+                for d in (1, 7):
+                    zz = (z + d) % 8
+                    send(ZNEAR, cent.at[:, pl.ds(pl.multiple_of(zz * 128, 128), 128)], tb.at[8 - d, c], sub=zz * 2 + c)
             l = lax.dot_general(cent[...], emb[k * RC:(k + 1) * RC, :], (((1,), (1,)), ((), ())),
                                 preferred_element_type=F32) - hn
             m = jnp.max(l, axis=0, keepdims=True)
@@ -124,9 +127,6 @@
             for core in range(2):
                 send(OVERZ, half, half, sub=((z + k) % 8) * 2 + core)
         send(OVERZ, half, half, sub=other)
-        for k in (1, 7):
-            zz = (z + k) % 8
-            send(ZNEAR, cent.at[:, pl.ds(pl.multiple_of(zz * 128, 128), 128)], tb.at[8 - k, c], sub=zz * 2 + c)
     with jax.named_scope("zwait"):
         drain(zbuf, rcv.at[ZFAR])
     with jax.named_scope("tabsend"):

time: 43.3 us -> 43.4 us (level)
  no operation moved by 1% of the time
where the time goes in v8:
time: 43.4 us; the launch traced here: 43.3 us
  Pallas kernels  42.5 us (98%)
  between operations  0.8 us (2%)
    pallas_call x1, Pallas kernels, shards(): pl.pallas_call(kernel, out_shape=(v((KL, D), F32), v((4, 16, 256), F32)),...  41.5 us
    pallas_call x1, Pallas kernels, shards(): pl.pallas_call(unload, out_shape=(hb((KL, D), F32), hb((4, 16, 256), F32)...  1.03 us

profile of v8, /device:TPU:1, one launch (start us, length us, event | category | flops | bytes accessed | tf_op | source)
XLA Modules:
  0.0 43.3 jit_solution(7320073541724083135)
XLA Ops:
  0.6 41.5 %step.1 = (f32[256,1024]{1,0:T(8,128)S(1)}, f32[4,16,256]{2,1,0:T(8,128)S(1)}) custom-call(bf16[3072,1024]{1,0:T(8,128)(2,1)} %emb_hbm.1, s32[3072]{0:T(1024)} %asg_hbm.1, bf16[256,1024]{1,0:T(8,128)(2,1)} %cent_hbm.1, f32[4,16,256]{2,1,0:T(8,128)} %cb_hbm.1), custom_call_target="tpu_custom_call" | custom-call | tf_op jit(solution)/shard_map/step/pallas_call | solution.py:400
  42.1 1.0 %unload.1 = (f32[256,1024]{1,0:T(8,128)}, f32[4,16,256]{2,1,0:T(8,128)}) custom-call(f32[256,1024]{1,0:T(8,128)S(1)} %get-tuple-element.4.cent_vm, f32[4,16,256]{2,1,0:T(8,128)S(1)} %get-tuple-element.5.code_vm), custom_call_target="tpu_custom_call" | custom-call | tf_op jit(solution)/shard_map/unload/pallas_call | solution.py:423

commit v9 on v7

--- a/solution.py
+++ b/solution.py
@@ -12,6 +12,8 @@
 SCALE = CENT + 8
 PHASES = SCALE + 4
 F32, BF16 = jnp.float32, jnp.bfloat16
+FAR_FIRST = sorted(
+    ((i % 4, i // 4) for i in range(1, 16)), key=lambda v: -sum(min(k, 4 - k) for k in v))
 LOG2E = 1.4426950408889634
 
 
@@ -43,6 +45,8 @@
     sub = lax.axis_index("sub")
     y, x = dp // 4, dp % 4
     z, c = sub // 2, sub % 2
+
+    others = [((y + ky) % 4) * 4 + (x + kx) % 4 for kx, ky in FAR_FIRST]
 
     def send(phase, src, dst, **where):
         rcopy(src, dst, snd.at[phase], rcv.at[phase], **where).start()
@@ -131,8 +135,8 @@
         drain(zbuf, rcv.at[ZFAR])
     with jax.named_scope("tabsend"):
         tb[2:7, c, rows16] = zbuf[...]
-        for j in range(1, 16):
-            send(TAB, zbuf, tb.at[2:7, c, rows16], dp=(dp + j) % 16)
+        for o in others:
+            send(TAB, zbuf, tb.at[2:7, c, rows16], dp=o)
     with jax.named_scope("finwait"):
         drain(cr.at[0:15, 0:12], rcv.at[OVERZ])
     with jax.named_scope("merge2"):
@@ -171,8 +175,8 @@
                 send(SWAP, tb.at[7, c], tb.at[7, c], sub=other)
     with jax.named_scope("counts"):
         cg[dp, 0:1, :] = jnp.sum(jnp.transpose(cp_), axis=0, keepdims=True)
-        for k in range(1, 16):
-            send(COUNT, cg.at[dp, 0:1], cg.at[dp, 0:1], dp=(dp + k) % 16)
+        for o in others:
+            send(COUNT, cg.at[dp, 0:1], cg.at[dp, 0:1], dp=o)
 
     with jax.named_scope("tabwait"):
         drain(tb.at[2:7, 0, 0:240], rcv.at[TAB])
@@ -340,8 +344,7 @@
             code(21 + s, 22 + s)
         prepare(3)
     with jax.named_scope("codeprep"):
-        for k in range(1, 16):
-            o = (dp + k) % 16
+        for o in others:
             send(CODE, cs.at[o, 0:9], cr.at[dp, 0:9], dp=o)
         cr[dp, 0:9, :] = cs[dp, 0:9, :]
     with jax.named_scope("s2B"):
@@ -359,9 +362,9 @@
         g8 = pl.ds(pl.multiple_of(go * 8, 8), 8)
         h128 = pl.ds(pl.multiple_of(ho * 128, 128), 128)
         cbo_ref[so, g8, h128] = (t + cb[so, g8, h128]) / (n + 1.0)
-        for k in range(1, 16):
+        for o in others:
             piece = cbo_ref.at[so, g8, h128]
-            send(NEWCODE, piece, piece, dp=(dp + k) % 16)
+            send(NEWCODE, piece, piece, dp=o)
     with jax.named_scope("newcent"):
         stage4(0)
         stage4(1)

time: 43.3 us -> 43.3 us (level)
  no operation moved by 1% of the time
where the time goes in v9:
time: 43.3 us; the launch traced here: 43.2 us
  Pallas kernels  42.4 us (98%)
  between operations  0.8 us (2%)
    pallas_call x1, Pallas kernels, shards(): pl.pallas_call(kernel, out_shape=(v((KL, D), F32), v((4, 16, 256), F32)),...  41.4 us
    pallas_call x1, Pallas kernels, shards(): pl.pallas_call(unload, out_shape=(hb((KL, D), F32), hb((4, 16, 256), F32)...  1.03 us

profile of v9, /device:TPU:1, one launch (start us, length us, event | category | flops | bytes accessed | tf_op | source)
XLA Modules:
  0.0 43.2 jit_solution(7893300417268964212)
XLA Ops:
  0.6 41.4 %step.1 = (f32[256,1024]{1,0:T(8,128)S(1)}, f32[4,16,256]{2,1,0:T(8,128)S(1)}) custom-call(bf16[3072,1024]{1,0:T(8,128)(2,1)} %emb_hbm.1, s32[3072]{0:T(1024)} %asg_hbm.1, bf16[256,1024]{1,0:T(8,128)(2,1)} %cent_hbm.1, f32[4,16,256]{2,1,0:T(8,128)} %cb_hbm.1), custom_call_target="tpu_custom_call" | custom-call | tf_op jit(solution)/shard_map/step/pallas_call | solution.py:403
  42.0 1.0 %unload.1 = (f32[256,1024]{1,0:T(8,128)}, f32[4,16,256]{2,1,0:T(8,128)}) custom-call(f32[256,1024]{1,0:T(8,128)S(1)} %get-tuple-element.4.cent_vm, f32[4,16,256]{2,1,0:T(8,128)S(1)} %get-tuple-element.5.code_vm), custom_call_target="tpu_custom_call" | custom-call | tf_op jit(solution)/shard_map/unload/pallas_call | solution.py:426
